TPU v7x, 128 devices: a whole 4x4x4 slice. The times are simulated.
128 devices in a mesh: space: 16 (over z_hi, x, core), chan: 8 (over y, z_lo).
Axes of the slice: x: 4, y: 4, z: 4 (z_hi: 2, z_lo: 2; z = z_hi * 2 + z_lo), core: 2. Of those that a mesh axis runs over, the one named last changes fastest.
Arguments:
- inputs: bfloat16 [128, 64, 32, 128], P('chan', 'space'), may hold values from -6 to 6
- filters: bfloat16 [27, 128, 128], P(None, 'chan'), may hold values from -0.109375 to 0.109375
- cotangent: bfloat16 [128, 64, 32, 128], P('chan', 'space'), may hold values from -6 to 6
Outputs:
- grad_inputs: bfloat16 [128, 64, 32, 128], P('chan', 'space')
- grad_filters: float32 [27, 128, 128], P(None, 'chan')
All inputs are finite; a program needn't handle non-finite values.
Results may differ from a plain program's by a relative error of at most 0.0049.
Values may be sent and summed in bfloat16 or wider, within the bound.
A program may use at most 128 MiB of HBM per device.

v0:
```python
import math

import jax
import jax.numpy as jnp
from jax import lax
from jax.sharding import PartitionSpec as P


def with_halo(block, sides, width):
    for axis, dim in sides:
        count = lax.axis_size(axis)
        forward = [(i, i + 1) for i in range(count - 1)]
        backward = [(target, source) for source, target in forward]
        low = lax.ppermute(
            lax.slice_in_dim(block, block.shape[dim] - width, None, axis=dim), axis, forward
        )
        high = lax.ppermute(lax.slice_in_dim(block, 0, width, axis=dim), axis, backward)
        block = jnp.concatenate([low, block, high], axis=dim)
    return block


def shifted(padded, depth_off, row_off, column_off, plane_count, row_count, column_count):
    return padded[
        :,
        depth_off : depth_off + plane_count,
        row_off : row_off + row_count,
        column_off : column_off + column_count,
    ]


def forward_part(padded, weights, plane_count, row_count, column_count):
    total = None
    for depth_off in range(3):
        stacked = jnp.concatenate(
            [
                shifted(
                    padded, depth_off, inner // 3, inner % 3, plane_count, row_count, column_count
                )
                for inner in range(9)
            ],
            axis=0,
        )
        block = weights[9 * depth_off : 9 * depth_off + 9].reshape(
            9 * weights.shape[1], weights.shape[2]
        )
        term = jnp.einsum("io,idhw->odhw", block, stacked, preferred_element_type=jnp.float32)
        total = term if total is None else total + term
    return total


def body(inputs, filters, cotangent):
    plane_count = inputs.shape[1]
    row_count = inputs.shape[2]
    column_count = inputs.shape[3]
    in_rim = with_halo(inputs, (("space", 1),), 1)
    in_pad = jnp.pad(in_rim, ((0, 0), (0, 0), (1, 1), (1, 1)))
    partial_sum = forward_part(in_pad, filters, plane_count, row_count, column_count)
    pre_act = lax.psum_scatter(partial_sum, "chan", scatter_dimension=0, tiled=True)
    sigma = jax.nn.sigmoid(pre_act)
    grad_out = (cotangent.astype(jnp.float32) * sigma * (1.0 + pre_act * (1.0 - sigma))).astype(
        jnp.bfloat16
    )
    grad_all = lax.all_gather(grad_out, "chan", axis=0, tiled=True)
    grad_rim = with_halo(grad_all, (("space", 1),), 1)
    grad_pad = jnp.pad(grad_rim, ((0, 0), (0, 0), (1, 1), (1, 1)))
    grad_in = None
    for offset in range(27):
        depth_off = offset // 9
        row_off = offset // 3 % 3
        column_off = offset % 3
        window = shifted(
            grad_pad,
            2 - depth_off,
            2 - row_off,
            2 - column_off,
            plane_count,
            row_count,
            column_count,
        )
        term = jnp.einsum(
            "io,odhw->idhw", filters[offset], window, preferred_element_type=jnp.float32
        )
        grad_in = term if grad_in is None else grad_in + term
    stacked_in = jnp.stack(
        [
            shifted(
                in_pad,
                offset // 9,
                offset // 3 % 3,
                offset % 3,
                plane_count,
                row_count,
                column_count,
            )
            for offset in range(27)
        ]
    )
    grad_w = jnp.einsum("kidhw,odhw->kio", stacked_in, grad_all, preferred_element_type=jnp.float32)
    grad_w = lax.psum(grad_w, "space")
    cell_total = plane_count * lax.axis_size("space") * row_count * column_count
    return (grad_in.astype(jnp.bfloat16), grad_w * (1.0 / math.sqrt(cell_total)))


def solution(mesh):
    placed = (P("chan", "space", None, None), P(None, "chan", None), P("chan", "space", None, None))
    return jax.shard_map(
        body,
        mesh=mesh,
        in_specs=placed,
        out_specs=(P("chan", "space", None, None), P(None, "chan", None)),
        check_vma=False,
    )
```

profile of v0, /device:TPU:1, one launch (start us, length us, event | category | flops | bytes accessed | tf_op | source)
XLA Modules:
  0.0 548.7 jit_solution(15890602798667119826)
XLA Ops:
  8.6 4.5 collective-permute-start
  13.1 1.9 collective-permute-start.1
  15.9 3.5 collective-permute-done.1
  26.4 2.5 fusion.245
  28.9 2.5 fusion.246
  31.3 5.7 %add_bitcast_fusion = f32[128,4,32,128]{0,3,2,1:T(8,128)} fusion(f32[4,32,128,128]{3,2,1,0:T(8,128)S(1)} %fusion.245, f32[4,32,128,128]{3,2,1,0:T(8,128)S(1)} %fusion.246, bf16[144,4,32,128]{3,0,2,1:T(8,128)(2,1)S(1)} %get-tuple-element.8, bf16[144,128,1,1]{1,0,3,2:T(8,128)(2,1)S(1)} %bitcast.324), kind=kOutput, calls=%fused_computation.12 | convolution fusion | flops 608174080 | bytes 29921280 | tf_op jit(solution)/shard_map/io,idhw->odhw/dot_general | solution.py:46
  37.0 10.7 %copy.48 = f32[128,4,32,128]{3,2,1,0:T(8,128)} copy(f32[128,4,32,128]{0,3,2,1:T(8,128)} %add_bitcast_fusion) | data formatting | bytes 16777216 | tf_op jit(solution)/shard_map/add | solution.py:47
  47.8 173.8 %reduce-scatter.2.cloned.1.call-done = f32[16,4,32,128]{3,2,1,0:T(8,128)} async-done(((f32[128,4,32,128]{3,2,1,0:T(8,128)}), f32[16,4,32,128]{3,2,1,0:T(8,128)}) %reduce-scatter.2.cloned.1.call-update) | async-done | bytes 1048592 | tf_op jit(solution)/shard_map/reduce_scatter | solution.py:58
  221.6 2.4 multiply_convert_fusion
  250.4 64.3 %all-gather.2.cloned.1.call-done = bf16[128,4,32,128]{3,2,1,0:T(8,128)(2,1)} async-done(((bf16[16,4,32,128]{3,2,1,0:T(8,128)(2,1)}), bf16[128,4,32,128]{3,2,1,0:T(8,128)(2,1)}) %all-gather.2.cloned.1.call-update) | async-done | bytes 4194320 | tf_op jit(solution)/shard_map/all_gather | solution.py:63
  314.7 5.0 copy.49
  319.8 2.0 copy-done
  323.0 2.7 collective-permute-start.3
  325.7 3.0 collective-permute-start.2
  328.7 7.8 %fusion.179 = f32[27,16,128]{2,1,0:T(8,128)} fusion(bf16[27,16,4,32,128]{4,1,3,2,0:T(8,128)(2,1)} %bitcast_dynamic-update-slice_fusion, bf16[128,4,32,128,1]{3,2,1,0,4:T(8,128)(2,1)S(1)} %bitcast.323), kind=kOutput, calls=%fused_computation.120 | convolution fusion | flops 1811939328 | bytes 18571264 | tf_op jit(solution)/shard_map/kidhw,odhw->kio/dot_general | solution.py:98
  336.6 5.5 %fusion.197 = f32[4,32,128,16]{2,3,1,0:T(8,128)} fusion(bf16[27,16,128]{2,1,0:T(8,128)(2,1)S(1)} %copy-done.11, bf16[128,4,32,128]{3,2,1,0:T(8,128)(2,1)} %all-gather.2.cloned.1.call-done), kind=kOutput, calls=%fused_computation.192 | convolution fusion | flops 67108864 | bytes 5246976 | tf_op jit(solution)/shard_map/io,odhw->idhw/dot_general | solution.py:80
  342.1 133.3 %all-reduce.4.cloned.1.call-done = f32[27,16,128]{2,1,0:T(8,128)} async-done(((f32[27,16,128]{2,1,0:T(8,128)}), f32[27,16,128]{2,1,0:T(8,128)}) %all-reduce.4.cloned.1.call-update) | async-done | bytes 221200 | tf_op jit(solution)/shard_map/psum | solution.py:99
  477.1 9.9 %select_maximum_fusion = bf16[128,6,34,130]{3,0,2,1:T(8,128)(2,1)S(1)} fusion(bf16[128,1,32,128]{3,0,2,1:T(8,128)(2,1)S(1)} %collective-permute-done.3, bf16[128,4,32,128]{3,0,2,1:T(8,128)(2,1)} %copy-done, bf16[128,1,32,128]{3,0,2,1:T(8,128)(2,1)S(1)} %collective-permute-done.2), kind=kLoop, calls=%fused_computation.7 | loop fusion | flops 64496640 | bytes 13080576 | tf_op jit(solution)/shard_map/concatenate | solution.py:18
  490.1 2.6 fusion.36
  492.7 2.5 fusion.38
  495.2 1.7 fusion.40
  496.9 2.5 fusion.42
  499.4 2.5 fusion.44
  501.9 1.7 fusion.46
  503.6 2.5 fusion.50
  506.1 1.7 fusion.52
  507.7 2.7 fusion.54
  517.8 2.5 fusion.85
  520.4 1.7 fusion.89
  522.0 2.5 fusion.92
  524.5 2.8 fusion.95
  530.5 6.3 %fusion.173 = f32[4,32,128,16]{2,3,1,0:T(8,128)S(1)} fusion(f32[4,32,128,16]{2,3,1,0:T(8,128)S(1)} %copy-done.4, f32[4,32,128,16]{2,3,1,0:T(8,128)S(1)} %fusion.32, f32[4,32,128,16]{2,3,1,0:T(8,128)} %fusion.34, f32[4,32,128,16]{2,3,1,0:T(8,128)} %fusion.36, f32[4,32,128,16]{2,3,1,0:T(8,128)} %fusion.38, f32[4,32,128,16]{2,3,1,0:T(8,128)} %fusion.40, ...), kind=kOutput, calls=%fused_computation.118 | convolution fusion | flops 70516736 | bytes 18878464 | tf_op jit(solution)/shard_map/io,odhw->idhw/dot_general | solution.py:80
  (87 shorter events, 57.0 us)
Async XLA Ops:
  7.2 214.4 %reduce-scatter.2.cloned.1.call-start = ((), (), s32[]{:S(2)}) async-start(), calls=%async_computation.1 | async-start | bytes 9437184 | tf_op jit(solution)/shard_map/reduce_scatter | solution.py:58
  8.6 7.3 %collective-permute-start = (bf16[16,1,32,128]{3,0,2,1:T(8,128)(2,1)S(1)}, bf16[16,1,32,128]{3,0,2,1:T(8,128)(2,1)S(1)}, u32[]{:S(2)}, u32[]{:S(2)}) collective-permute-start(bf16[16,1,32,128]{3,0,2,1:T(8,128)(2,1)S(1)} %get-tuple-element.34), channel_id=1, source_target_pairs={{0,8},{8,16},{16,24},{24,32},{32,40},{40,48},{48,56},{56,64},{64,7... | collective-permute-start | bytes 393224 | tf_op jit(solution)/shard_map/ppermute | solution.py:14
  13.1 6.3 %collective-permute-start.1 = (bf16[16,1,32,128]{3,0,2,1:T(8,128)(2,1)S(1)}, bf16[16,1,32,128]{3,0,2,1:T(8,128)(2,1)S(1)}, u32[]{:S(2)}, u32[]{:S(2)}) collective-permute-start(bf16[16,1,32,128]{3,0,2,1:T(8,128)(2,1)S(1)} %get-tuple-element.35), channel_id=1, source_target_pairs={{8,0},{16,8},{24,16},{32,24},{40,32},{48,40},{56,48},{64,56},{72,6... | collective-permute-start | bytes 393224 | tf_op jit(solution)/shard_map/ppermute | solution.py:17
  20.7 2.0 copy-start.3
  47.7 173.9 %copy-start.10 = (bf16[16,4,32,128]{3,2,1,0:T(8,128)(2,1)S(1)}, bf16[16,4,32,128]{3,2,1,0:T(8,128)(2,1)}, u32[]{:S(2)}) copy-start(bf16[16,4,32,128]{3,2,1,0:T(8,128)(2,1)} %param.5) | copy-start | bytes 1572868
  47.7 267.0 %all-gather.2.cloned.1.call-start = ((), (), s32[]{:S(2)}) async-start(), calls=%async_computation.2 | async-start | bytes 4718592 | tf_op jit(solution)/shard_map/all_gather | solution.py:63
  224.0 251.4 %all-reduce.4.cloned.1.call-start = ((), (), s32[]{:S(2)}) async-start(), calls=%async_computation.3 | async-start | bytes 442368 | tf_op jit(solution)/shard_map/psum | solution.py:99
  314.7 14.0 %copy-start.2 = (bf16[128,4,32,128]{3,2,1,0:T(8,128)(2,1)S(1)}, bf16[128,4,32,128]{3,2,1,0:T(8,128)(2,1)}, u32[]{:S(2)}) copy-start(bf16[128,4,32,128]{3,2,1,0:T(8,128)(2,1)} %all-gather.2.cloned.1.call-done) | copy-start | bytes 12582916
  319.8 2.0 copy-start
  323.0 154.1 %collective-permute-start.3 = (bf16[128,1,32,128]{3,0,2,1:T(8,128)(2,1)}, bf16[128,1,32,128]{3,0,2,1:T(8,128)(2,1)S(1)}, u32[]{:S(2)}, u32[]{:S(2)}) collective-permute-start(bf16[128,1,32,128]{3,0,2,1:T(8,128)(2,1)} %get-tuple-element.7), channel_id=1, source_target_pairs={{8,0},{16,8},{24,16},{32,24},{40,32},{48,40},{56,48},{64,56},{72,6... | collective-permute-start | bytes 3145736 | tf_op jit(solution)/shard_map/ppermute | solution.py:17
  325.7 151.4 %collective-permute-start.2 = (bf16[128,1,32,128]{3,0,2,1:T(8,128)(2,1)S(1)}, bf16[128,1,32,128]{3,0,2,1:T(8,128)(2,1)S(1)}, u32[]{:S(2)}, u32[]{:S(2)}) collective-permute-start(bf16[128,1,32,128]{3,0,2,1:T(8,128)(2,1)S(1)} %get-tuple-element.6), channel_id=1, source_target_pairs={{0,8},{8,16},{16,24},{24,32},{32,40},{40,48},{48,56},{56,64},{64,7... | collective-permute-start | bytes 3145736 | tf_op jit(solution)/shard_map/ppermute | solution.py:14
  328.7 7.9 %copy-start.11 = (bf16[27,16,128]{2,1,0:T(8,128)(2,1)S(1)}, bf16[27,16,128]{2,1,0:T(8,128)(2,1)}, u32[]{:S(2)}) copy-start(bf16[27,16,128]{2,1,0:T(8,128)(2,1)} %param.4) | copy-start | bytes 331780
  524.5 4.4 copy-start.1
  527.3 3.3 copy-start.4
  536.8 1.2 copy-start.5
  536.9 1.5 copy-start.6
  536.9 1.8 copy-start.7
  536.9 2.1 copy-start.8
  536.9 2.5 copy-start.9
Sparse Core Ops, SparseCore 0:
  47.8 173.6 reduce-scatter.1
  224.2 90.5 all-gather.1
  336.7 138.6 all-reduce.3
where the time goes:
time: 558 us; the launch traced here: 549 us
  waiting for transfers between devices  375 us (67%)
  matrix products  75.9 us (14%)
  local copies, waits for them, and re-layouts  53.7 us (10%)
  other arithmetic  17.3 us (3%)
  between operations  14.5 us (3%)
  starting transfers between devices  12.3 us (2%)
    reduce_scatter x1, waiting for transfers between devices, body(): lax.psum_scatter(partial_sum, 'chan', scatter_dimension=0, tiled=True)  174 us
    psum x1, waiting for transfers between devices, body(): grad_w = lax.psum(grad_w, 'space')  133 us
    all_gather x1, waiting for transfers between devices, body(): grad_all = lax.all_gather(grad_out, 'chan', axis=0, tiled=True)  64.3 us
    dot_general x27, matrix products, body(): jnp.einsum('io,odhw->idhw', filters[offset], window, preferred_element_ty...  57.4 us
    unnamed x57, local copies, waits for them, and re-layouts  34.1 us
  transfers between devices with their start and end apart: 7, of which 4 were waited for; matrix products, arithmetic and copies ran while one was open for 8% of the time, Pallas kernels for 0%

commit v1 on v0

v1 whole, which is shorter than its diff:
```python
import math

import jax
import jax.numpy as jnp
from jax import lax
from jax.experimental import pallas as pl
from jax.experimental.pallas import tpu as pltpu
from jax.sharding import PartitionSpec as P

MESH = pl.DeviceIdType.MESH
BF16 = jnp.bfloat16
F32 = jnp.float32
PITCH = 136


def row_block(c):
    y = lax.div(c, 2)
    z = lax.rem(c, 2)
    q = lax.rem(y, 2)
    return 2 * y + z + q - 2 * z * q


def remote(src, dst, send_sem, recv_sem, **where):
    return pltpu.make_async_remote_copy(
        src_ref=src, dst_ref=dst, send_sem=send_sem, recv_sem=recv_sem,
        device_id=where, device_id_type=MESH,
    )


def shift_lanes(block, by):
    lane = lax.broadcasted_iota(jnp.int32, (block.shape[0], 128), 1)
    edge = 0 if by == 1 else 127
    pieces = []
    for d in range(block.shape[1] // 128):
        rolled = pltpu.roll(block[:, 128 * d : 128 * d + 128], by % 128, 1)
        pieces.append(jnp.where(lane == edge, 0.0, rolled))
    return jnp.concatenate(pieces, axis=1)


def kernel(
    scale, x_ref, f_ref, t_ref, gi_ref, gw_ref,
    wide, xt, tt, ws, xb, ct, wg, wf, gb, gs, gw, gwb, abuf, sb, bbuf, cb, cbuf, gwf, gout, back,
    x_s, x_r, t_s, t_r, w_s, w_r, xh_s, xh_r, gh_s, gh_r, gi_s, gi_r,
    a_s, a_r, b_s, b_r, c_s, c_r, d_s, d_r,
):
    c = lax.axis_index("chan")
    g = lax.axis_index("space")
    r = row_block(c)
    core = lax.rem(g, 2)
    chip = lax.div(g, 2)
    mine = pl.ds(pl.multiple_of(16 * c, 16), 16)
    has_lo, has_hi = g > 0, g < 15
    has_up, has_down = r > 0, r < 7

    barrier = pltpu.get_barrier_semaphore()
    for k in range(1, 8):
        pl.semaphore_signal(barrier, inc=1, device_id={"chan": lax.rem(c + k, 8)}, device_id_type=MESH)
    for k in range(1, 16):
        pl.semaphore_signal(barrier, inc=1, device_id={"space": lax.rem(g + k, 16)}, device_id_type=MESH)
    for dg, has_g in ((-1, has_lo), (1, has_hi)):
        for dr, has_r in ((-1, has_up), (1, has_down)):
            both = jnp.logical_and(has_g, has_r)

            @pl.when(both)
            def _():
                pl.semaphore_signal(
                    barrier, inc=1,
                    device_id={"space": g + dg, "chan": row_block(r + dr)}, device_id_type=MESH,
                )

    xt[0] = jnp.zeros((16, 512), BF16)
    xt[33] = jnp.zeros((16, 512), BF16)

    @pl.when(g == 0)
    def _():
        xb[:, :, 0:128] = jnp.zeros((6, 128, 128), BF16)
        gb[:, :, 0:128] = jnp.zeros((6, 128, 128), BF16)

    @pl.when(g == 15)
    def _():
        xb[:, :, 640:768] = jnp.zeros((6, 128, 128), BF16)
        gb[:, :, 640:768] = jnp.zeros((6, 128, 128), BF16)

    @pl.when(r == 0)
    def _():
        gb[0] = jnp.zeros((128, 768), BF16)

    @pl.when(r == 7)
    def _():
        gb[5] = jnp.zeros((128, 768), BF16)

    for tap in range(27):
        a, b, cc = tap // 9, tap // 3 % 3, tap % 3
        at = 128 * (3 * (2 - a) + 2 - b)
        ws[cc, :, at : at + 128] = f_ref[tap]

    def to_rows(src, dst, first):
        for ch in range(16):
            wide[PITCH * ch : PITCH * ch + 128, :] = src[ch].reshape(128, 128).astype(F32)

        def step(h, _):
            for d in range(4):
                rows = wide[pl.ds(32 * d + h, 16, stride=PITCH), :]
                dst[first + h, :, 128 * d : 128 * d + 128] = rows.astype(BF16)
            return 0

        lax.fori_loop(0, 32, step, 0)

    to_rows(x_ref, xt, 1)

    sides_g = has_lo.astype(jnp.int32) + has_hi.astype(jnp.int32)
    sides_r = has_up.astype(jnp.int32) + has_down.astype(jnp.int32)
    pl.semaphore_wait(barrier, 22 + sides_g * sides_r)

    x_copies, w_copies, t_copies = [], [], []
    for k in range(1, 8):
        to = lax.rem(c + k, 8)
        x_copies.append(remote(
            xt.at[pl.ds(4 * row_block(to), 6)], xb.at[:, mine, 128:640],
            x_s.at[k - 1], x_r.at[k - 1], chan=to,
        ))
        x_copies[-1].start()
    for k in range(1, 8):
        to = lax.rem(c + k, 8)
        w_copies.append(remote(ws, wg.at[:, mine, :], w_s.at[k - 1], w_r.at[k - 1], chan=to))
        w_copies[-1].start()
    xb[:, mine, 128:640] = xt[pl.ds(4 * r, 6)]
    wg[:, mine, :] = ws[...]

    to_rows(t_ref, tt, 0)
    for k in range(1, 8):
        to = lax.rem(c + k, 8)
        t_copies.append(remote(
            tt.at[pl.ds(4 * row_block(to), 4)], ct.at[:, mine, :],
            t_s.at[k - 1], t_r.at[k - 1], chan=to,
        ))
        t_copies[-1].start()
    ct[:, mine, :] = tt[pl.ds(4 * r, 4)]

    for copy in x_copies:
        copy.wait_recv()
    lo_copy = remote(xb.at[:, :, 128:256], xb.at[:, :, 640:768], xh_s.at[0], xh_r.at[0], space=g - 1)
    hi_copy = remote(xb.at[:, :, 512:640], xb.at[:, :, 0:128], xh_s.at[1], xh_r.at[1], space=g + 1)
    pl.when(has_lo)(lambda: lo_copy.start())
    pl.when(has_hi)(lambda: hi_copy.start())

    for copy in w_copies:
        copy.wait_recv()
    for tap in range(27):
        a, b, cc = tap // 9, tap // 3 % 3, tap % 3
        at = 128 * (3 * (2 - a) + 2 - b)
        to = 128 * (3 * a + b)
        wf[128 * cc : 128 * cc + 128, to : to + 128] = wg[cc, :, at : at + 128].T

    pl.when(has_hi)(lambda: lo_copy.wait_recv())
    pl.when(has_lo)(lambda: hi_copy.wait_recv())
    for copy in t_copies:
        copy.wait_recv()

    def patches(src, h):
        rows = [src[h + b, :, 128 * a : 128 * a + 512] for a in range(3) for b in range(3)]
        return jnp.concatenate(rows, axis=0)

    def forward(h, _):
        acc = jnp.dot(wf[...], patches(xb, h), preferred_element_type=F32)
        pre = shift_lanes(acc[0:128], 1) + acc[128:256] + shift_lanes(acc[256:384], -1)
        sigma = 1.0 / (1.0 + jnp.exp(-pre))
        grad = ct[h].astype(F32) * sigma * (1.0 + pre * (1.0 - sigma))
        gb[h + 1, :, 128:640] = grad.astype(BF16)
        gs[h, 0:128, :] = shift_lanes(grad, -1).astype(BF16)
        gs[h, 128:256, :] = grad.astype(BF16)
        gs[h, 256:384, :] = shift_lanes(grad, 1).astype(BF16)
        return 0

    lax.fori_loop(0, 4, forward, 0)

    up, down = row_block(lax.max(r - 1, 0)), row_block(lax.min(r + 1, 7))
    rims = [
        (gb.at[1:5, :, 128:256], gb.at[1:5, :, 640:768], has_lo, has_hi, {"space": g - 1}),
        (gb.at[1:5, :, 512:640], gb.at[1:5, :, 0:128], has_hi, has_lo, {"space": g + 1}),
        (gb.at[1, :, 128:640], gb.at[5, :, 128:640], has_up, has_down, {"chan": up}),
        (gb.at[4, :, 128:640], gb.at[0, :, 128:640], has_down, has_up, {"chan": down}),
    ]
    for dg, plane, to_plane in ((-1, 128, 640), (1, 512, 0)):
        for dr, row, to_row in ((-1, 1, 5), (1, 4, 0)):
            has_g, from_g = (has_lo, has_hi) if dg < 0 else (has_hi, has_lo)
            has_r, from_r = (has_up, has_down) if dr < 0 else (has_down, has_up)
            rims.append((
                gb.at[row, :, plane : plane + 128], gb.at[to_row, :, to_plane : to_plane + 128],
                jnp.logical_and(has_g, has_r), jnp.logical_and(from_g, from_r),
                {"space": g + dg, "chan": up if dr < 0 else down},
            ))
    g_copies = []
    for n, (src, dst, sends, gets, where) in enumerate(rims):
        copy = remote(src, dst, gh_s.at[n], gh_r.at[n], **where)
        g_copies.append((copy, sends, gets))
        pl.when(sends)(copy.start)

    grads = jnp.concatenate([gs[h] for h in range(4)], axis=1)
    for tap in range(9):
        a, b = tap // 3, tap % 3
        rows = jnp.concatenate([xb[h + b, :, 128 * a : 128 * a + 512] for h in range(4)], axis=1)
        part = lax.dot_general(rows, grads, (((1,), (1,)), ((), ())), preferred_element_type=F32)
        for cc in range(3):
            gw[3 * tap + cc] = part[:, 128 * cc : 128 * cc + 128]
            gwb[3 * tap + cc] = part[:, 128 * cc : 128 * cc + 128].astype(BF16)
    for tap in range(27, 32):
        gw[tap] = jnp.zeros((128, 128), F32)
        gwb[tap] = jnp.zeros((128, 128), BF16)

    a_copy = remote(
        gwb.at[pl.ds(16 * (1 - core), 16)], abuf, a_s.at[0], a_r.at[0], space=g + 1 - 2 * core
    )
    a_copy.start()

    for copy, _, gets in g_copies:
        pl.when(gets)(copy.wait_recv)

    def backward(h, _):
        weights = jnp.concatenate([wg[cc] for cc in range(3)], axis=0)
        acc = jnp.dot(weights, patches(gb, h), preferred_element_type=F32)
        total = shift_lanes(acc[0:128], -1) + acc[128:256] + shift_lanes(acc[256:384], 1)
        gout[h] = total.astype(BF16)
        return 0

    gi_copies = []
    lax.fori_loop(0, 4, backward, 0)
    for k in range(1, 8):
        to = lax.rem(c + k, 8)
        gi_copies.append(remote(
            gout.at[:, pl.ds(pl.multiple_of(16 * to, 16), 16), :], back.at[pl.ds(4 * r, 4)],
            gi_s.at[k - 1], gi_r.at[k - 1], chan=to,
        ))
        gi_copies[-1].start()
    back[pl.ds(4 * r, 4)] = gout[:, mine, :]

    a_copy.wait_recv()
    sb[...] = (gw[pl.ds(16 * core, 16)] + abuf[...].astype(F32)).astype(BF16)
    b_copies = []
    for k in range(1, 8):
        to = lax.rem(c + k, 8)
        b_copies.append(remote(
            sb.at[:, pl.ds(pl.multiple_of(16 * to, 16), 16), :], bbuf.at[k - 1],
            b_s.at[k - 1], b_r.at[k - 1], chan=to,
        ))
        b_copies[-1].start()
    total = sb[:, mine, :].astype(F32)
    for k in range(7):
        b_copies[k].wait_recv()
        total = total + bbuf[k].astype(F32)
    cb[...] = total.astype(BF16)
    c_copies = []
    for k in range(1, 8):
        to = lax.rem(chip + k, 8)
        c_copies.append(remote(
            cb.at[pl.ds(2 * to, 2)], cbuf.at[k - 1], c_s.at[k - 1], c_r.at[k - 1],
            space=2 * to + core,
        ))
        c_copies[-1].start()
    total = cb[pl.ds(2 * chip, 2)].astype(F32)
    for k in range(7):
        c_copies[k].wait_recv()
        total = total + cbuf[k].astype(F32)
    piece = pl.ds(16 * core + 2 * chip, 2)
    gwf[piece] = total * scale
    d_copies = []
    for k in range(1, 16):
        d_copies.append(remote(
            gwf.at[piece], gwf.at[piece], d_s.at[k - 1], d_r.at[k - 1],
            space=lax.rem(g + k, 16),
        ))
        d_copies[-1].start()

    for copy in gi_copies:
        copy.wait_recv()
    for d in range(4):
        for h in range(32):
            wide[24 * h : 24 * h + 16, :] = back[h, :, 128 * d : 128 * d + 128].astype(F32)

        def step(ch, _):
            gi_ref[ch, d] = wide[pl.ds(ch, 32, stride=24), :].astype(BF16)
            return 0

        lax.fori_loop(0, 16, step, 0)

    for copy in d_copies:
        copy.wait_recv()
    gw_ref[...] = gwf[0:27]

    for copy in x_copies + w_copies + t_copies + gi_copies + b_copies + c_copies + d_copies:
        copy.wait_send()
    a_copy.wait_send()
    pl.when(has_lo)(lo_copy.wait_send)
    pl.when(has_hi)(hi_copy.wait_send)
    for copy, sends, _ in g_copies:
        pl.when(sends)(copy.wait_send)


def body(inputs, filters, cotangent):
    cells = inputs.shape[1] * lax.axis_size("space") * inputs.shape[2] * inputs.shape[3]
    scale = 1.0 / math.sqrt(cells)
    sems = [7, 7, 7, 7, 7, 7, 2, 2, 8, 8, 7, 7, 1, 1, 7, 7, 7, 7, 15, 15]
    scratch = [
        ((PITCH * 16, 128), F32),
        ((34, 16, 512), BF16),
        ((32, 16, 512), BF16),
        ((3, 16, 1152), BF16),
        ((6, 128, 768), BF16),
        ((4, 128, 512), BF16),
        ((3, 128, 1152), BF16),
        ((384, 1152), BF16),
        ((6, 128, 768), BF16),
        ((4, 384, 512), BF16),
        ((32, 128, 128), F32),
        ((32, 128, 128), BF16),
        ((16, 128, 128), BF16),
        ((16, 128, 128), BF16),
        ((7, 16, 16, 128), BF16),
        ((16, 16, 128), BF16),
        ((7, 2, 16, 128), BF16),
        ((32, 16, 128), F32),
        ((4, 128, 512), BF16),
        ((32, 16, 512), BF16),
    ]
    vmem = pl.BlockSpec(memory_space=pltpu.VMEM)
    return pl.pallas_call(
        lambda *refs: kernel(scale, *refs),
        out_shape=(
            jax.ShapeDtypeStruct(inputs.shape, BF16),
            jax.ShapeDtypeStruct(filters.shape, F32),
        ),
        in_specs=[vmem] * 3,
        out_specs=(vmem, vmem),
        scratch_shapes=[pltpu.VMEM(s, t) for s, t in scratch]
        + [pltpu.SemaphoreType.DMA((n,)) for n in sems],
        compiler_params=pltpu.CompilerParams(
            collective_id=0, has_side_effects=True, vmem_limit_bytes=60 * 2**20
        ),
        name="conv_backward",
    )(inputs, filters, cotangent)


def solution(mesh):
    placed = (P("chan", "space", None, None), P(None, "chan", None), P("chan", "space", None, None))
    return jax.shard_map(
        body,
        mesh=mesh,
        in_specs=placed,
        out_specs=(P("chan", "space", None, None), P(None, "chan", None)),
        check_vma=False,
    )
```

time: 558 us -> 81.2 us (0.15); the launches traced: 549 us -> 81 us
  waiting for transfers between devices: 375 us -> 0 us
  Pallas kernels: 0 us -> 77.8 us
  matrix products: 75.9 us -> 0 us
  local copies, waits for them, and re-layouts: 53.7 us -> 2.61 us
  other arithmetic: 17.3 us -> 0 us
  between operations: 14.5 us -> 0.65 us
  starting transfers between devices: 12.3 us -> 0 us
    reduce_scatter x1 -> x0, waiting for transfers between devices: 174 us -> none  [body(): lax.psum_scatter(partial_sum, 'chan', scatter_dimension=0, tiled=True)]
    psum x1 -> x0, waiting for transfers between devices: 133 us -> none  [body(): grad_w = lax.psum(grad_w, 'space')]
    pallas_call x0 -> x1, Pallas kernels: none -> 77.8 us  [body(): pl.pallas_call(lambda *refs: kernel(scale, *refs), out_shape=(jax.ShapeDt...]
    dot_general x31 -> x0, matrix products: 75.9 us -> none  [the longest x27 57.4 us: body(): jnp.einsum('io,odhw->idhw', filters[offset], window, preferred_element_ty...]
    all_gather x1 -> x0, waiting for transfers between devices: 64.3 us -> none  [body(): grad_all = lax.all_gather(grad_out, 'chan', axis=0, tiled=True)]
    unnamed x57 -> x4, local copies, waits for them, and re-layouts: 34.1 us -> 2.61 us
    ppermute x4 -> x0, starting transfers between devices: 12.1 us -> none  [the longest x2 7.49 us: with_halo(): lax.ppermute(lax.slice_in_dim(block, block.shape[dim] - width, None, axis...]
    concatenate x2 -> x0, other arithmetic: 10.9 us -> none  [with_halo(): block = jnp.concatenate([low, block, high], axis=dim)]
  transfers between devices with their start and end apart: 7 -> 0, of which waited for: 4 -> 0; matrix products, arithmetic and copies ran while one was open for 8% -> 0% of each run, Pallas kernels for 0% -> 0%
where the time goes in v1:
time: 81.2 us; the launch traced here: 81 us
  Pallas kernels  77.8 us (96%)
  local copies, waits for them, and re-layouts  2.61 us (3%)
    pallas_call x1, Pallas kernels, body(): pl.pallas_call(lambda *refs: kernel(scale, *refs), out_shape=(jax.ShapeDt...  77.8 us
    unnamed x4, local copies, waits for them, and re-layouts  2.61 us

profile of v1, /device:TPU:1, one launch (start us, length us, event | category | flops | bytes accessed | tf_op | source)
XLA Modules:
  0.0 81.0 jit_solution(8934284665272156563)
XLA Ops:
  0.6 77.8 %conv_backward.1 = (bf16[16,4,32,128]{3,2,1,0:T(8,128)(2,1)}, f32[27,16,128]{2,1,0:T(8,128)}) custom-call(bf16[16,4,32,128]{3,2,1,0:T(8,128)(2,1)} %refs_0_.1, bf16[27,16,128]{2,1,0:T(8,128)(2,1)} %refs_1_.1, bf16[16,4,32,128]{3,2,1,0:T(8,128)(2,1)} %refs_2_.1), custom_call_target="tpu_custom_call" | custom-call | tf_op jit(solution)/shard_map/conv_backward/pallas_call | solution.py:326
  78.4 0.0 copy-start
  78.4 1.9 %copy.7 = bf16[16,4,32,128]{3,2,1,0:T(8,128)(2,1)} copy(bf16[16,4,32,128]{3,2,1,0:T(8,128)(2,1)} %get-tuple-element.4) | data formatting | bytes 1048576
  80.4 0.0 copy-done
  80.4 0.7 copy.8
Async XLA Ops:
  78.4 1.9 %copy-start = (f32[27,16,128]{2,1,0:T(8,128)S(1)}, f32[27,16,128]{2,1,0:T(8,128)}, u32[]{:S(2)}) copy-start(f32[27,16,128]{2,1,0:T(8,128)} %get-tuple-element.5) | copy-start | bytes 663556

commit v2 on v1

v2 whole, which is shorter than its diff:
```python
import math

import jax
import jax.numpy as jnp
from jax import lax
from jax.experimental import pallas as pl
from jax.experimental.pallas import tpu as pltpu
from jax.sharding import PartitionSpec as P

MESH = pl.DeviceIdType.MESH
BF16 = jnp.bfloat16
F32 = jnp.float32
PITCH = 136


def row_block(c):
    y = lax.div(c, 2)
    z = lax.rem(c, 2)
    q = lax.rem(y, 2)
    return 2 * y + z + q - 2 * z * q


class Copy:
    def __init__(self, src, dst, send_sem, recv_sem, where, sends=None, gets=None):
        self.copy = pltpu.make_async_remote_copy(
            src_ref=src, dst_ref=dst, send_sem=send_sem, recv_sem=recv_sem,
            device_id=where, device_id_type=MESH,
        )
        self.sends, self.gets = sends, gets

    def start(self):
        self.copy.start() if self.sends is None else pl.when(self.sends)(self.copy.start)
        return self

    def wait_recv(self):
        self.copy.wait_recv() if self.gets is None else pl.when(self.gets)(self.copy.wait_recv)

    def wait_send(self):
        self.copy.wait_send() if self.sends is None else pl.when(self.sends)(self.copy.wait_send)


def shift_lanes(block, by):
    lane = lax.broadcasted_iota(jnp.int32, (block.shape[0], 128), 1)
    edge = 0 if by == 1 else 127
    pieces = []
    for d in range(block.shape[1] // 128):
        rolled = pltpu.roll(block[:, 128 * d : 128 * d + 128], by % 128, 1)
        pieces.append(jnp.where(lane == edge, 0.0, rolled))
    return jnp.concatenate(pieces, axis=1)


def kernel(
    scale, x_ref, f_ref, t_ref, gi_ref, gw_ref,
    wide, xt, tt, fp, xb, ct, wall, wg, wf, pre, gb, gs, gw, gwb, abuf, sb, xbuf, yb, ybuf, gwf,
    gout, back,
    x_s, x_r, t_s, t_r, wy_s, wy_r, wx_s, wx_r, wd_s, wd_r, xh_s, xh_r, gh_s, gh_r, gi_s, gi_r,
    a_s, a_r, b_s, b_r, y_s, y_r, d_s, d_r,
):
    c = lax.axis_index("chan")
    g = lax.axis_index("space")
    r = row_block(c)
    core = lax.rem(g, 2)
    px = lax.rem(lax.div(g, 2), 4)
    pz = lax.div(g, 8)
    sibling = g + 1 - 2 * core
    mine = pl.ds(pl.multiple_of(16 * c, 16), 16)
    has_lo, has_hi = g > 0, g < 15
    has_up, has_down = r > 0, r < 7

    def chan_peer(k):
        return lax.rem(c + k, 8)

    def x_peer(k):
        return 8 * pz + 2 * lax.rem(px + k, 4) + core

    barrier = pltpu.get_barrier_semaphore()
    for k in range(1, 8):
        pl.semaphore_signal(barrier, inc=1, device_id={"chan": chan_peer(k)}, device_id_type=MESH)
    for k in range(1, 16):
        pl.semaphore_signal(barrier, inc=1, device_id={"space": lax.rem(g + k, 16)}, device_id_type=MESH)
    for k in range(1, 8):
        pl.semaphore_signal(
            barrier, inc=1, device_id={"space": lax.rem(g + 8, 16), "chan": chan_peer(k)},
            device_id_type=MESH,
        )
    for dg, has_g in ((-1, has_lo), (1, has_hi)):
        for dr, has_r in ((-1, has_up), (1, has_down)):

            @pl.when(jnp.logical_and(has_g, has_r))
            def _():
                pl.semaphore_signal(
                    barrier, inc=1,
                    device_id={"space": g + dg, "chan": row_block(r + dr)}, device_id_type=MESH,
                )

    xt[0] = jnp.zeros((16, 512), BF16)
    xt[33] = jnp.zeros((16, 512), BF16)

    @pl.when(g == 0)
    def _():
        xb[:, :, 0:128] = jnp.zeros((6, 128, 128), BF16)
        gb[:, :, 0:128] = jnp.zeros((6, 128, 128), BF16)

    @pl.when(g == 15)
    def _():
        xb[:, :, 640:768] = jnp.zeros((6, 128, 128), BF16)
        gb[:, :, 640:768] = jnp.zeros((6, 128, 128), BF16)

    @pl.when(r == 0)
    def _():
        gb[0] = jnp.zeros((128, 768), BF16)

    @pl.when(r == 7)
    def _():
        gb[5] = jnp.zeros((128, 768), BF16)

    fp[0:27] = f_ref[...]
    fp[27:32] = jnp.zeros((5, 16, 128), BF16)

    def to_rows(src, dst, first):
        for ch in range(16):
            wide[PITCH * ch : PITCH * ch + 128, :] = src[ch].reshape(128, 128).astype(F32)

        def step(h, _):
            for d in range(4):
                rows = wide[pl.ds(32 * d + h, 16, stride=PITCH), :]
                dst[first + h, :, 128 * d : 128 * d + 128] = rows.astype(BF16)
            return 0

        lax.fori_loop(0, 32, step, 0)

    to_rows(x_ref, xt, 1)
    sides_g = has_lo.astype(jnp.int32) + has_hi.astype(jnp.int32)
    sides_r = has_up.astype(jnp.int32) + has_down.astype(jnp.int32)
    pl.semaphore_wait(barrier, 29 + sides_g * sides_r)

    part = 4 * (4 * core + px)
    wy_copies = [
        Copy(
            fp.at[pl.ds(part, 4)], wall.at[pl.ds(part, 4), mine, :],
            wy_s.at[k - 1], wy_r.at[k - 1], {"chan": chan_peer(k)},
        ).start()
        for k in range(1, 8)
    ]
    wall[pl.ds(part, 4), mine, :] = fp[pl.ds(part, 4)]
    x_copies = [
        Copy(
            xt.at[pl.ds(4 * row_block(chan_peer(k)), 6)], xb.at[:, mine, 128:640],
            x_s.at[k - 1], x_r.at[k - 1], {"chan": chan_peer(k)},
        ).start()
        for k in range(1, 8)
    ]
    xb[:, mine, 128:640] = xt[pl.ds(4 * r, 6)]
    to_rows(t_ref, tt, 0)
    t_copies = [
        Copy(
            tt.at[pl.ds(4 * row_block(chan_peer(k)), 4)], ct.at[:, mine, :],
            t_s.at[k - 1], t_r.at[k - 1], {"chan": chan_peer(k)},
        ).start()
        for k in range(1, 8)
    ]
    ct[:, mine, :] = tt[pl.ds(4 * r, 4)]
    for copy in wy_copies:
        copy.wait_recv()
    wx_copies = [
        Copy(
            wall.at[pl.ds(part, 4)], wall.at[pl.ds(part, 4)],
            wx_s.at[k - 1], wx_r.at[k - 1], {"space": x_peer(k)},
        ).start()
        for k in range(1, 4)
    ]
    wd_copies = []
    for k in range(4):
        if k:
            wx_copies[k - 1].wait_recv()
        piece = wall.at[pl.ds(4 * (4 * core + lax.rem(px + 4 - k, 4)), 4)]
        wd_copies.append(
            Copy(piece, piece, wd_s.at[k], wd_r.at[k], {"space": sibling}).start()
        )

    for copy in x_copies:
        copy.wait_recv()
    h_copies = [
        Copy(xb.at[:, :, 128:256], xb.at[:, :, 640:768], xh_s.at[0], xh_r.at[0],
             {"space": g - 1}, has_lo, has_hi).start(),
        Copy(xb.at[:, :, 512:640], xb.at[:, :, 0:128], xh_s.at[1], xh_r.at[1],
             {"space": g + 1}, has_hi, has_lo).start(),
    ]
    for copy in wd_copies:
        copy.wait_recv()
    for tap in range(27):
        a, b, cc = tap // 9, tap // 3 % 3, tap % 3
        block = wall[tap]
        rows = slice(128 * cc, 128 * cc + 128)
        wg[rows, 128 * (8 - 3 * a - b) : 128 * (9 - 3 * a - b)] = block
        wf[rows, 128 * (3 * a + b) : 128 * (3 * a + b + 1)] = block.T
    for copy in h_copies:
        copy.wait_recv()

    def patches(src, h):
        rows = [src[h + b, :, 128 * a : 128 * a + 512] for a in range(3) for b in range(3)]
        return jnp.concatenate(rows, axis=0)

    def forward(h, _):
        acc = jnp.dot(wf[...], patches(xb, h), preferred_element_type=F32)
        pre[h] = shift_lanes(acc[0:128], 1) + acc[128:256] + shift_lanes(acc[256:384], -1)
        return 0

    lax.fori_loop(0, 4, forward, 0)
    for copy in t_copies:
        copy.wait_recv()

    up, down = row_block(lax.max(r - 1, 0)), row_block(lax.min(r + 1, 7))
    row_rims, plane_rims = [], []

    def send_rims(row, to_row, has_r, from_r, to):
        n = 3 * len(row_rims)
        sent = [Copy(
            gb.at[row, :, 128:640], gb.at[to_row, :, 128:640], gh_s.at[n], gh_r.at[n],
            {"chan": to}, has_r, from_r,
        ).start()]
        for m, plane, to_plane, dg in ((1, 128, 640, -1), (2, 512, 0, 1)):
            has_g, from_g = (has_lo, has_hi) if dg < 0 else (has_hi, has_lo)
            sent.append(Copy(
                gb.at[row, :, plane : plane + 128], gb.at[to_row, :, to_plane : to_plane + 128],
                gh_s.at[n + m], gh_r.at[n + m], {"space": g + dg, "chan": to},
                jnp.logical_and(has_g, has_r), jnp.logical_and(from_g, from_r),
            ).start())
        row_rims.append(sent)

    for h in (0, 3, 1, 2):
        p = pre[h]
        sigma = 1.0 / (1.0 + jnp.exp(-p))
        grad = ct[h].astype(F32) * sigma * (1.0 + p * (1.0 - sigma))
        gb[h + 1, :, 128:640] = grad.astype(BF16)
        if h == 0:
            send_rims(1, 5, has_up, has_down, up)
        if h == 3:
            send_rims(4, 0, has_down, has_up, down)
        gs[h, 0:128, :] = shift_lanes(grad, -1).astype(BF16)
        gs[h, 128:256, :] = grad.astype(BF16)
        gs[h, 256:384, :] = shift_lanes(grad, 1).astype(BF16)
    plane_rims = [
        Copy(gb.at[1:5, :, 128:256], gb.at[1:5, :, 640:768], gh_s.at[6], gh_r.at[6],
             {"space": g - 1}, has_lo, has_hi).start(),
        Copy(gb.at[1:5, :, 512:640], gb.at[1:5, :, 0:128], gh_s.at[7], gh_r.at[7],
             {"space": g + 1}, has_hi, has_lo).start(),
    ]

    grads = jnp.concatenate([gs[h] for h in range(4)], axis=1)
    for tap in range(9):
        a, b = tap // 3, tap % 3
        rows = jnp.concatenate([xb[h + b, :, 128 * a : 128 * a + 512] for h in range(4)], axis=1)
        prod = lax.dot_general(rows, grads, (((1,), (1,)), ((), ())), preferred_element_type=F32)
        for cc in range(3):
            gw[3 * tap + cc] = prod[:, 128 * cc : 128 * cc + 128]
            gwb[3 * tap + cc] = prod[:, 128 * cc : 128 * cc + 128].astype(BF16)
    for tap in range(27, 32):
        gw[tap] = jnp.zeros((128, 128), F32)
        gwb[tap] = jnp.zeros((128, 128), BF16)

    a_copy = Copy(
        gwb.at[pl.ds(16 * (1 - core), 16)], abuf, a_s.at[0], a_r.at[0], {"space": sibling}
    ).start()

    gi_copies = []

    def backward(h):
        acc = jnp.dot(wg[...], patches(gb, h), preferred_element_type=F32)
        total = shift_lanes(acc[0:128], -1) + acc[128:256] + shift_lanes(acc[256:384], 1)
        gout[h] = total.astype(BF16)

    def send_rows(first, count, n):
        for k in range(1, 8):
            to = pl.ds(pl.multiple_of(16 * chan_peer(k), 16), 16)
            gi_copies.append(Copy(
                gout.at[pl.ds(first, count), to, :], back.at[pl.ds(4 * r + first, count)],
                gi_s.at[7 * n + k - 1], gi_r.at[7 * n + k - 1], {"chan": chan_peer(k)},
            ).start())
        back[pl.ds(4 * r + first, count)] = gout[first : first + count, mine, :]

    for copy in plane_rims:
        copy.wait_recv()
    backward(1)
    backward(2)
    send_rows(1, 2, 0)

    a_copy.wait_recv()
    sb[...] = (gw[pl.ds(16 * core, 16)] + abuf[...].astype(F32)).astype(BF16)
    b_copies = [
        Copy(
            sb.at[pl.ds(4 * lax.rem(px + k, 4), 4)], xbuf.at[k - 1], b_s.at[k - 1], b_r.at[k - 1],
            {"space": x_peer(k)},
        ).start()
        for k in range(1, 4)
    ]
    for sent in row_rims:
        for copy in sent:
            copy.wait_recv()
    backward(0)
    send_rows(0, 1, 1)
    backward(3)
    send_rows(3, 1, 2)

    total = sb[pl.ds(4 * px, 4)].astype(F32)
    for k in range(3):
        b_copies[k].wait_recv()
        total = total + xbuf[k].astype(F32)
    yb[...] = total.astype(BF16)
    y_copies = []
    for dz in range(2):
        for k in range(8):
            if dz or k:
                z, to = lax.rem(pz + dz, 2), chan_peer(k)
                n = 8 * dz + k - 1
                y_copies.append(Copy(
                    yb.at[pl.ds(2 * z, 2), pl.ds(pl.multiple_of(16 * to, 16), 16), :], ybuf.at[n],
                    y_s.at[n], y_r.at[n], {"space": 8 * z + 2 * px + core, "chan": to},
                ).start())
    total = yb[pl.ds(2 * pz, 2), mine, :].astype(F32)
    for n in range(15):
        y_copies[n].wait_recv()
        total = total + ybuf[n].astype(F32)
    piece = pl.ds(16 * core + 4 * px + 2 * pz, 2)
    gwf[piece] = total * scale
    d_copies = [
        Copy(
            gwf.at[piece], gwf.at[piece], d_s.at[k - 1], d_r.at[k - 1],
            {"space": lax.rem(g + k, 16)},
        ).start()
        for k in range(1, 16)
    ]
    for copy in gi_copies:
        copy.wait_recv()
    for d in range(4):
        for h in range(32):
            wide[24 * h : 24 * h + 16, :] = back[h, :, 128 * d : 128 * d + 128].astype(F32)

        def step(ch, _):
            gi_ref[ch, d] = wide[pl.ds(ch, 32, stride=24), :].astype(BF16)
            return 0

        lax.fori_loop(0, 16, step, 0)
    for copy in d_copies:
        copy.wait_recv()
    gw_ref[...] = gwf[0:27]

    copies = wy_copies + x_copies + t_copies + wx_copies + wd_copies + h_copies + row_rims[0]
    copies += row_rims[1] + plane_rims + [a_copy] + gi_copies + b_copies + y_copies + d_copies
    for copy in copies:
        copy.wait_send()


def body(inputs, filters, cotangent):
    cells = inputs.shape[1] * lax.axis_size("space") * inputs.shape[2] * inputs.shape[3]
    scale = 1.0 / math.sqrt(cells)
    pairs = [7, 7, 7, 3, 4, 2, 8, 21, 1, 3, 15, 15]
    scratch = [
        ((PITCH * 16, 128), F32),
        ((34, 16, 512), BF16),
        ((32, 16, 512), BF16),
        ((32, 16, 128), BF16),
        ((6, 128, 768), BF16),
        ((4, 128, 512), BF16),
        ((32, 128, 128), BF16),
        ((384, 1152), BF16),
        ((384, 1152), BF16),
        ((4, 128, 512), F32),
        ((6, 128, 768), BF16),
        ((4, 384, 512), BF16),
        ((32, 128, 128), F32),
        ((32, 128, 128), BF16),
        ((16, 128, 128), BF16),
        ((16, 128, 128), BF16),
        ((3, 4, 128, 128), BF16),
        ((4, 128, 128), BF16),
        ((15, 2, 16, 128), BF16),
        ((32, 16, 128), F32),
        ((4, 128, 512), BF16),
        ((32, 16, 512), BF16),
    ]
    vmem = pl.BlockSpec(memory_space=pltpu.VMEM)
    return pl.pallas_call(
        lambda *refs: kernel(scale, *refs),
        out_shape=(
            jax.ShapeDtypeStruct(inputs.shape, BF16),
            jax.ShapeDtypeStruct(filters.shape, F32),
        ),
        in_specs=[vmem] * 3,
        out_specs=(vmem, vmem),
        scratch_shapes=[pltpu.VMEM(s, t) for s, t in scratch]
        + [pltpu.SemaphoreType.DMA((n,)) for n in pairs for _ in range(2)],
        compiler_params=pltpu.CompilerParams(
            collective_id=0, has_side_effects=True, vmem_limit_bytes=60 * 2**20
        ),
        name="conv_backward",
    )(inputs, filters, cotangent)


def solution(mesh):
    placed = (P("chan", "space", None, None), P(None, "chan", None), P("chan", "space", None, None))
    return jax.shard_map(
        body,
        mesh=mesh,
        in_specs=placed,
        out_specs=(P("chan", "space", None, None), P(None, "chan", None)),
        check_vma=False,
    )
```

time: 81.2 us -> 66 us (0.81)
  Pallas kernels: 77.8 us -> 62.6 us
    pallas_call x1, Pallas kernels: 77.8 us -> 62.6 us  [body(): pl.pallas_call(lambda *refs: kernel(scale, *refs), out_shape=(jax.ShapeDt...]
where the time goes in v2:
time: 66 us; the launch traced here: 65.9 us
  Pallas kernels  62.6 us (95%)
  local copies, waits for them, and re-layouts  2.61 us (4%)
    pallas_call x1, Pallas kernels, body(): pl.pallas_call(lambda *refs: kernel(scale, *refs), out_shape=(jax.ShapeDt...  62.6 us
    unnamed x4, local copies, waits for them, and re-layouts  2.61 us

profile of v2, /device:TPU:1, one launch (start us, length us, event | category | flops | bytes accessed | tf_op | source)
XLA Modules:
  0.0 65.9 jit_solution(17108655282478626604)
XLA Ops:
  0.6 62.6 %conv_backward.1 = (bf16[16,4,32,128]{3,2,1,0:T(8,128)(2,1)}, f32[27,16,128]{2,1,0:T(8,128)}) custom-call(bf16[16,4,32,128]{3,2,1,0:T(8,128)(2,1)} %refs_0_.1, bf16[27,16,128]{2,1,0:T(8,128)(2,1)} %refs_1_.1, bf16[16,4,32,128]{3,2,1,0:T(8,128)(2,1)} %refs_2_.1), custom_call_target="tpu_custom_call" | custom-call | tf_op jit(solution)/shard_map/conv_backward/pallas_call | solution.py:383
  63.3 0.0 copy-start
  63.3 1.9 %copy.7 = bf16[16,4,32,128]{3,2,1,0:T(8,128)(2,1)} copy(bf16[16,4,32,128]{3,2,1,0:T(8,128)(2,1)} %get-tuple-element.4) | data formatting | bytes 1048576
  65.2 0.0 copy-done
  65.2 0.7 %copy.8 = f32[27,16,128]{2,1,0:T(8,128)} copy(f32[27,16,128]{2,1,0:T(8,128)S(1)} %copy-done) | data formatting | bytes 442368
Async XLA Ops:
  63.3 1.9 %copy-start = (f32[27,16,128]{2,1,0:T(8,128)S(1)}, f32[27,16,128]{2,1,0:T(8,128)}, u32[]{:S(2)}) copy-start(f32[27,16,128]{2,1,0:T(8,128)} %get-tuple-element.5) | copy-start | bytes 663556

commit v3 on v2

--- a/solution.py
+++ b/solution.py
@@ -11,6 +11,7 @@
 BF16 = jnp.bfloat16
 F32 = jnp.float32
 PITCH = 136
+STEPS = (2, 1, 3, 0)
 
 
 def row_block(c):
@@ -50,11 +51,11 @@
 
 
 def kernel(
-    scale, x_ref, f_ref, t_ref, gi_ref, gw_ref,
-    wide, xt, tt, fp, xb, ct, wall, wg, wf, pre, gb, gs, gw, gwb, abuf, sb, xbuf, yb, ybuf, gwf,
+    scale, x_hbm, f_hbm, t_hbm, gi_hbm, gw_hbm,
+    x_ref, f_ref, t_ref, gi_ref, gw_ref, wide, xt, tt, fp, xb, ct, wall, wg, wf, pre, gb, gs, gw, gwb, abuf, sb, xbuf, yb, ybuf, gwf,
     gout, back,
     x_s, x_r, t_s, t_r, wy_s, wy_r, wx_s, wx_r, wd_s, wd_r, xh_s, xh_r, gh_s, gh_r, gi_s, gi_r,
-    a_s, a_r, b_s, b_r, y_s, y_r, d_s, d_r,
+    a_s, a_r, b_s, b_r, y_s, y_r, d_s, d_r, io_sem,
 ):
     c = lax.axis_index("chan")
     g = lax.axis_index("space")
@@ -73,16 +74,25 @@
     def x_peer(k):
         return 8 * pz + 2 * lax.rem(px + k, 4) + core
 
+    def half_peer(k):
+        return 8 * pz + lax.rem(2 * px + core + k, 8)
+
     barrier = pltpu.get_barrier_semaphore()
     for k in range(1, 8):
         pl.semaphore_signal(barrier, inc=1, device_id={"chan": chan_peer(k)}, device_id_type=MESH)
-    for k in range(1, 16):
-        pl.semaphore_signal(barrier, inc=1, device_id={"space": lax.rem(g + k, 16)}, device_id_type=MESH)
     for k in range(1, 8):
+        pl.semaphore_signal(barrier, inc=1, device_id={"space": half_peer(k)}, device_id_type=MESH)
+    for k in range(8):
         pl.semaphore_signal(
             barrier, inc=1, device_id={"space": lax.rem(g + 8, 16), "chan": chan_peer(k)},
             device_id_type=MESH,
         )
+    for edge, dg in ((7, 1), (8, -1)):
+
+        @pl.when(g == edge)
+        def _():
+            pl.semaphore_signal(barrier, inc=1, device_id={"space": g + dg}, device_id_type=MESH)
+
     for dg, has_g in ((-1, has_lo), (1, has_hi)):
         for dr, has_r in ((-1, has_up), (1, has_down)):
 
@@ -93,6 +103,13 @@
                     device_id={"space": g + dg, "chan": row_block(r + dr)}, device_id_type=MESH,
                 )
 
+    loads = [
+        pltpu.make_async_copy(src, dst, io_sem.at[n])
+        for n, (src, dst) in enumerate(((x_hbm, x_ref), (f_hbm, f_ref), (t_hbm, t_ref)))
+    ]
+    for load in loads:
+        load.start()
+
     xt[0] = jnp.zeros((16, 512), BF16)
     xt[33] = jnp.zeros((16, 512), BF16)
 
@@ -114,8 +131,6 @@
     def _():
         gb[5] = jnp.zeros((128, 768), BF16)
 
-    fp[0:27] = f_ref[...]
-    fp[27:32] = jnp.zeros((5, 16, 128), BF16)
 
     def to_rows(src, dst, first):
         for ch in range(16):
@@ -129,16 +144,22 @@
 
         lax.fori_loop(0, 32, step, 0)
 
+    loads[0].wait()
     to_rows(x_ref, xt, 1)
     sides_g = has_lo.astype(jnp.int32) + has_hi.astype(jnp.int32)
     sides_r = has_up.astype(jnp.int32) + has_down.astype(jnp.int32)
-    pl.semaphore_wait(barrier, 29 + sides_g * sides_r)
+    middle = (g == 7).astype(jnp.int32) + (g == 8).astype(jnp.int32)
+    loads[1].wait()
+    fp[0:27] = f_ref[...]
+    fp[27:32] = jnp.zeros((5, 16, 128), BF16)
+    pl.semaphore_wait(barrier, 22 + middle + sides_g * sides_r)
 
     part = 4 * (4 * core + px)
+    some = part < 28
     wy_copies = [
         Copy(
             fp.at[pl.ds(part, 4)], wall.at[pl.ds(part, 4), mine, :],
-            wy_s.at[k - 1], wy_r.at[k - 1], {"chan": chan_peer(k)},
+            wy_s.at[k - 1], wy_r.at[k - 1], {"chan": chan_peer(k)}, some, some,
         ).start()
         for k in range(1, 8)
     ]
@@ -151,6 +172,7 @@
         for k in range(1, 8)
     ]
     xb[:, mine, 128:640] = xt[pl.ds(4 * r, 6)]
+    loads[2].wait()
     to_rows(t_ref, tt, 0)
     t_copies = [
         Copy(
@@ -166,17 +188,10 @@
         Copy(
             wall.at[pl.ds(part, 4)], wall.at[pl.ds(part, 4)],
             wx_s.at[k - 1], wx_r.at[k - 1], {"space": x_peer(k)},
+            some, core + lax.rem(px + 4 - k, 4) < 4,
         ).start()
         for k in range(1, 4)
     ]
-    wd_copies = []
-    for k in range(4):
-        if k:
-            wx_copies[k - 1].wait_recv()
-        piece = wall.at[pl.ds(4 * (4 * core + lax.rem(px + 4 - k, 4)), 4)]
-        wd_copies.append(
-            Copy(piece, piece, wd_s.at[k], wd_r.at[k], {"space": sibling}).start()
-        )
 
     for copy in x_copies:
         copy.wait_recv()
@@ -186,6 +201,16 @@
         Copy(xb.at[:, :, 512:640], xb.at[:, :, 0:128], xh_s.at[1], xh_r.at[1],
              {"space": g + 1}, has_hi, has_lo).start(),
     ]
+    wd_copies = []
+    for k in range(4):
+        if k:
+            wx_copies[k - 1].wait_recv()
+        owner = lax.rem(px + 4 - k, 4)
+        piece = wall.at[pl.ds(4 * (4 * core + owner), 4)]
+        wd_copies.append(Copy(
+            piece, piece, wd_s.at[k], wd_r.at[k], {"space": sibling},
+            core + owner < 4, 1 - core + owner < 4,
+        ).start())
     for copy in wd_copies:
         copy.wait_recv()
     for tap in range(27):
@@ -248,20 +273,44 @@
     ]
 
     grads = jnp.concatenate([gs[h] for h in range(4)], axis=1)
-    for tap in range(9):
-        a, b = tap // 3, tap % 3
-        rows = jnp.concatenate([xb[h + b, :, 128 * a : 128 * a + 512] for h in range(4)], axis=1)
-        prod = lax.dot_general(rows, grads, (((1,), (1,)), ((), ())), preferred_element_type=F32)
+
+    def product(ab):
+        lanes = pl.ds(pl.multiple_of(128 * lax.div(ab, 3), 128), 512)
+        rows = jnp.concatenate([xb[h + lax.rem(ab, 3), :, lanes] for h in range(4)], axis=1)
+        return lax.dot_general(rows, grads, (((1,), (1,)), ((), ())), preferred_element_type=F32)
+
+    ninth = product(jnp.int32(8))
+    for n in range(8):
+        last = ninth[:, 128 * n : 128 * n + 128] if n < 3 else jnp.zeros((128, 128), F32)
+        gw[n, 3] = last
+        gwb[n, 3] = last.astype(BF16)
+    a_copies, b_copies = [], []
+
+    def pair_sum(j):
+        a_copies[j].wait_recv()
+        q = lax.rem(px + STEPS[j], 4)
+        total = gw[4 * core + q] + abuf[j].astype(F32)
+        if STEPS[j] == 0:
+            return total
+        sb[j] = total.astype(BF16)
+        b_copies.append(Copy(
+            sb.at[j], xbuf.at[j], b_s.at[j], b_r.at[j], {"space": x_peer(STEPS[j])}
+        ).start())
+
+    for j in range(4):
+        q = lax.rem(px + STEPS[j], 4)
+        other, own = 4 * (1 - core) + q, 4 * core + q
+        prod = product(other)
         for cc in range(3):
-            gw[3 * tap + cc] = prod[:, 128 * cc : 128 * cc + 128]
-            gwb[3 * tap + cc] = prod[:, 128 * cc : 128 * cc + 128].astype(BF16)
-    for tap in range(27, 32):
-        gw[tap] = jnp.zeros((128, 128), F32)
-        gwb[tap] = jnp.zeros((128, 128), BF16)
-
-    a_copy = Copy(
-        gwb.at[pl.ds(16 * (1 - core), 16)], abuf, a_s.at[0], a_r.at[0], {"space": sibling}
-    ).start()
+            gwb[other, cc] = prod[:, 128 * cc : 128 * cc + 128].astype(BF16)
+        a_copies.append(Copy(
+            gwb.at[other], abuf.at[j], a_s.at[j], a_r.at[j], {"space": sibling}
+        ).start())
+        prod = product(own)
+        for cc in range(3):
+            gw[own, cc] = prod[:, 128 * cc : 128 * cc + 128]
+        if j:
+            pair_sum(j - 1)
 
     gi_copies = []
 
@@ -285,15 +334,6 @@
     backward(2)
     send_rows(1, 2, 0)
 
-    a_copy.wait_recv()
-    sb[...] = (gw[pl.ds(16 * core, 16)] + abuf[...].astype(F32)).astype(BF16)
-    b_copies = [
-        Copy(
-            sb.at[pl.ds(4 * lax.rem(px + k, 4), 4)], xbuf.at[k - 1], b_s.at[k - 1], b_r.at[k - 1],
-            {"space": x_peer(k)},
-        ).start()
-        for k in range(1, 4)
-    ]
     for sent in row_rims:
         for copy in sent:
             copy.wait_recv()
@@ -302,10 +342,10 @@
     backward(3)
     send_rows(3, 1, 2)
 
-    total = sb[pl.ds(4 * px, 4)].astype(F32)
-    for k in range(3):
-        b_copies[k].wait_recv()
-        total = total + xbuf[k].astype(F32)
+    total = pair_sum(3)
+    for j in range(3):
+        b_copies[j].wait_recv()
+        total = total + xbuf[j].astype(F32)
     yb[...] = total.astype(BF16)
     y_copies = []
     for dz in range(2):
@@ -314,21 +354,20 @@
                 z, to = lax.rem(pz + dz, 2), chan_peer(k)
                 n = 8 * dz + k - 1
                 y_copies.append(Copy(
-                    yb.at[pl.ds(2 * z, 2), pl.ds(pl.multiple_of(16 * to, 16), 16), :], ybuf.at[n],
+                    yb.at[:, pl.ds(pl.multiple_of(16 * to, 16), 16), :], ybuf.at[8 * pz + c],
                     y_s.at[n], y_r.at[n], {"space": 8 * z + 2 * px + core, "chan": to},
                 ).start())
-    total = yb[pl.ds(2 * pz, 2), mine, :].astype(F32)
-    for n in range(15):
-        y_copies[n].wait_recv()
+    ybuf[8 * pz + c] = yb[:, mine, :]
+    for copy in y_copies:
+        copy.wait_recv()
+    total = ybuf[0].astype(F32)
+    for n in range(1, 16):
         total = total + ybuf[n].astype(F32)
-    piece = pl.ds(16 * core + 4 * px + 2 * pz, 2)
-    gwf[piece] = total * scale
+    piece = gwf.at[4 * core + px]
+    piece[...] = total.astype(BF16)
     d_copies = [
-        Copy(
-            gwf.at[piece], gwf.at[piece], d_s.at[k - 1], d_r.at[k - 1],
-            {"space": lax.rem(g + k, 16)},
-        ).start()
-        for k in range(1, 16)
+        Copy(piece, piece, d_s.at[k - 1], d_r.at[k - 1], {"space": half_peer(k)}).start()
+        for k in range(1, 8)
     ]
     for copy in gi_copies:
         copy.wait_recv()
@@ -341,21 +380,34 @@
             return 0
 
         lax.fori_loop(0, 16, step, 0)
+    out = pltpu.make_async_copy(gi_ref, gi_hbm, io_sem.at[0])
+    out.start()
     for copy in d_copies:
         copy.wait_recv()
-    gw_ref[...] = gwf[0:27]
+    for tap in range(27):
+        n, slot = (tap // 3, tap % 3) if tap < 24 else (tap - 24, 3)
+        gw_ref[tap] = gwf[n, slot].astype(F32) * scale
+    out_w = pltpu.make_async_copy(gw_ref, gw_hbm, io_sem.at[1])
+    out_w.start()
 
     copies = wy_copies + x_copies + t_copies + wx_copies + wd_copies + h_copies + row_rims[0]
-    copies += row_rims[1] + plane_rims + [a_copy] + gi_copies + b_copies + y_copies + d_copies
+    copies += row_rims[1] + plane_rims + a_copies + gi_copies + b_copies + y_copies + d_copies
     for copy in copies:
         copy.wait_send()
+    out.wait()
+    out_w.wait()
 
 
 def body(inputs, filters, cotangent):
     cells = inputs.shape[1] * lax.axis_size("space") * inputs.shape[2] * inputs.shape[3]
     scale = 1.0 / math.sqrt(cells)
-    pairs = [7, 7, 7, 3, 4, 2, 8, 21, 1, 3, 15, 15]
+    pairs = [7, 7, 7, 3, 4, 2, 8, 21, 4, 3, 15, 7]
     scratch = [
+        (inputs.shape, BF16),
+        (filters.shape, BF16),
+        (inputs.shape, BF16),
+        (inputs.shape, BF16),
+        (filters.shape, F32),
         ((PITCH * 16, 128), F32),
         ((34, 16, 512), BF16),
         ((32, 16, 512), BF16),
@@ -368,28 +420,29 @@
         ((4, 128, 512), F32),
         ((6, 128, 768), BF16),
         ((4, 384, 512), BF16),
-        ((32, 128, 128), F32),
-        ((32, 128, 128), BF16),
-        ((16, 128, 128), BF16),
-        ((16, 128, 128), BF16),
+        ((8, 4, 128, 128), F32),
+        ((8, 4, 128, 128), BF16),
+        ((4, 4, 128, 128), BF16),
+        ((3, 4, 128, 128), BF16),
         ((3, 4, 128, 128), BF16),
         ((4, 128, 128), BF16),
-        ((15, 2, 16, 128), BF16),
-        ((32, 16, 128), F32),
+        ((16, 4, 16, 128), BF16),
+        ((8, 4, 16, 128), BF16),
         ((4, 128, 512), BF16),
         ((32, 16, 512), BF16),
     ]
-    vmem = pl.BlockSpec(memory_space=pltpu.VMEM)
+    hbm = pl.BlockSpec(memory_space=pl.ANY)
     return pl.pallas_call(
         lambda *refs: kernel(scale, *refs),
         out_shape=(
             jax.ShapeDtypeStruct(inputs.shape, BF16),
             jax.ShapeDtypeStruct(filters.shape, F32),
         ),
-        in_specs=[vmem] * 3,
-        out_specs=(vmem, vmem),
+        in_specs=[hbm] * 3,
+        out_specs=(hbm, hbm),
         scratch_shapes=[pltpu.VMEM(s, t) for s, t in scratch]
-        + [pltpu.SemaphoreType.DMA((n,)) for n in pairs for _ in range(2)],
+        + [pltpu.SemaphoreType.DMA((n,)) for n in pairs for _ in range(2)]
+        + [pltpu.SemaphoreType.DMA((3,))],
         compiler_params=pltpu.CompilerParams(
             collective_id=0, has_side_effects=True, vmem_limit_bytes=60 * 2**20
         ),

time: 66 us -> 60.1 us (0.911)
  Pallas kernels: 62.6 us -> 56.7 us
    pallas_call x1, Pallas kernels: 62.6 us -> 56.7 us  [body(): pl.pallas_call(lambda *refs: kernel(scale, *refs), out_shape=(jax.ShapeDt...]
where the time goes in v3:
time: 60.1 us; the launch traced here: 60 us
  Pallas kernels  56.7 us (94%)
  local copies, waits for them, and re-layouts  2.61 us (4%)
  between operations  0.65 us (1%)
    pallas_call x1, Pallas kernels, body(): pl.pallas_call(lambda *refs: kernel(scale, *refs), out_shape=(jax.ShapeDt...  56.7 us
    unnamed x4, local copies, waits for them, and re-layouts  2.61 us

profile of v3, /device:TPU:1, one launch (start us, length us, event | category | flops | bytes accessed | tf_op | source)
XLA Modules:
  0.0 60.0 jit_solution(2966227347496690179)
XLA Ops:
  0.6 56.7 %conv_backward.1 = (bf16[16,4,32,128]{3,2,1,0:T(8,128)(2,1)}, f32[27,16,128]{2,1,0:T(8,128)}) custom-call(bf16[16,4,32,128]{3,2,1,0:T(8,128)(2,1)} %refs_0_.1, bf16[27,16,128]{2,1,0:T(8,128)(2,1)} %refs_1_.1, bf16[16,4,32,128]{3,2,1,0:T(8,128)(2,1)} %refs_2_.1), custom_call_target="tpu_custom_call" | custom-call | tf_op jit(solution)/shard_map/conv_backward/pallas_call | solution.py:435
  57.4 0.0 copy-start
  57.4 1.9 %copy.7 = bf16[16,4,32,128]{3,2,1,0:T(8,128)(2,1)} copy(bf16[16,4,32,128]{3,2,1,0:T(8,128)(2,1)} %get-tuple-element.4) | data formatting | bytes 1048576
  59.3 0.0 copy-done
  59.3 0.7 %copy.8 = f32[27,16,128]{2,1,0:T(8,128)} copy(f32[27,16,128]{2,1,0:T(8,128)S(1)} %copy-done) | data formatting | bytes 442368
Async XLA Ops:
  57.4 1.9 %copy-start = (f32[27,16,128]{2,1,0:T(8,128)S(1)}, f32[27,16,128]{2,1,0:T(8,128)}, u32[]{:S(2)}) copy-start(f32[27,16,128]{2,1,0:T(8,128)} %get-tuple-element.5) | copy-start | bytes 663556

commit v4 on v3

--- a/solution.py
+++ b/solution.py
@@ -38,6 +38,11 @@
 
     def wait_send(self):
         self.copy.wait_send() if self.sends is None else pl.when(self.sends)(self.copy.wait_send)
+
+
+def drain(like, sem, when=None):
+    wait = pltpu.make_async_copy(like, like, sem).wait
+    wait() if when is None else pl.when(when)(wait)
 
 
 def shift_lanes(block, by):
@@ -52,10 +57,11 @@
 
 def kernel(
     scale, x_hbm, f_hbm, t_hbm, gi_hbm, gw_hbm,
-    x_ref, f_ref, t_ref, gi_ref, gw_ref, wide, xt, tt, fp, xb, ct, wall, wg, wf, pre, gb, gs, gw, gwb, abuf, sb, xbuf, yb, ybuf, gwf,
+    x_ref, f_ref, t_ref, gi_ref, gw_ref, wide, xt, tt, fp, xb, ct, wall, wg, wf, pre, gb, gs, gw, gwb, abuf, sb, xbuf,
+    gw9, gwb9, abuf9, sb9, xbuf9, yb, ybuf, gwf,
     gout, back,
     x_s, x_r, t_s, t_r, wy_s, wy_r, wx_s, wx_r, wd_s, wd_r, xh_s, xh_r, gh_s, gh_r, gi_s, gi_r,
-    a_s, a_r, b_s, b_r, y_s, y_r, d_s, d_r, io_sem,
+    a_s, a_r, a9_s, a9_r, b_s, b_r, b9_s, b9_r, y_s, y_r, d_s, d_r, io_sem,
 ):
     c = lax.axis_index("chan")
     g = lax.axis_index("space")
@@ -159,7 +165,7 @@
     wy_copies = [
         Copy(
             fp.at[pl.ds(part, 4)], wall.at[pl.ds(part, 4), mine, :],
-            wy_s.at[k - 1], wy_r.at[k - 1], {"chan": chan_peer(k)}, some, some,
+            wy_s, wy_r, {"chan": chan_peer(k)}, some, some,
         ).start()
         for k in range(1, 8)
     ]
@@ -167,7 +173,7 @@
     x_copies = [
         Copy(
             xt.at[pl.ds(4 * row_block(chan_peer(k)), 6)], xb.at[:, mine, 128:640],
-            x_s.at[k - 1], x_r.at[k - 1], {"chan": chan_peer(k)},
+            x_s, x_r.at[k - 1], {"chan": chan_peer(k)},
         ).start()
         for k in range(1, 8)
     ]
@@ -177,50 +183,64 @@
     t_copies = [
         Copy(
             tt.at[pl.ds(4 * row_block(chan_peer(k)), 4)], ct.at[:, mine, :],
-            t_s.at[k - 1], t_r.at[k - 1], {"chan": chan_peer(k)},
+            t_s, t_r, {"chan": chan_peer(k)},
         ).start()
         for k in range(1, 8)
     ]
     ct[:, mine, :] = tt[pl.ds(4 * r, 4)]
-    for copy in wy_copies:
-        copy.wait_recv()
+    drain(fp.at[0:28], wy_r, some)
     wx_copies = [
         Copy(
             wall.at[pl.ds(part, 4)], wall.at[pl.ds(part, 4)],
-            wx_s.at[k - 1], wx_r.at[k - 1], {"space": x_peer(k)},
+            wx_s, wx_r.at[k - 1], {"space": x_peer(k)},
             some, core + lax.rem(px + 4 - k, 4) < 4,
         ).start()
         for k in range(1, 4)
     ]
 
-    for copy in x_copies:
-        copy.wait_recv()
-    h_copies = [
-        Copy(xb.at[:, :, 128:256], xb.at[:, :, 640:768], xh_s.at[0], xh_r.at[0],
-             {"space": g - 1}, has_lo, has_hi).start(),
-        Copy(xb.at[:, :, 512:640], xb.at[:, :, 0:128], xh_s.at[1], xh_r.at[1],
-             {"space": g + 1}, has_hi, has_lo).start(),
-    ]
     wd_copies = []
-    for k in range(4):
-        if k:
-            wx_copies[k - 1].wait_recv()
+
+    def pass_filters(k):
         owner = lax.rem(px + 4 - k, 4)
         piece = wall.at[pl.ds(4 * (4 * core + owner), 4)]
         wd_copies.append(Copy(
-            piece, piece, wd_s.at[k], wd_r.at[k], {"space": sibling},
+            piece, piece, wd_s, wd_r, {"space": sibling},
             core + owner < 4, 1 - core + owner < 4,
         ).start())
-    for copy in wd_copies:
-        copy.wait_recv()
+
+    pass_filters(0)
+
+    h_copies = []
+
+    def pass_rims(k):
+        rows = pl.ds(pl.multiple_of(16 * lax.rem(c + 8 - k, 8), 16), 16)
+        for n, at, to, dg in ((0, 128, 640, -1), (1, 512, 0, 1)):
+            has_g, from_g = (has_lo, has_hi) if dg < 0 else (has_hi, has_lo)
+            h_copies.append(Copy(
+                xb.at[:, rows, at : at + 128], xb.at[:, rows, to : to + 128],
+                xh_s.at[n], xh_r.at[n], {"space": g + dg}, has_g, from_g,
+            ).start())
+
+    pass_rims(0)
+    for k in range(1, 6):
+        x_copies[k - 1].wait_recv()
+        pass_rims(k)
+    for k in range(1, 4):
+        wx_copies[k - 1].wait_recv()
+        pass_filters(k)
+    for k in range(6, 8):
+        x_copies[k - 1].wait_recv()
+        pass_rims(k)
+    drain(wall.at[0:12], wd_r, core == 0)
+    drain(wall.at[0:16], wd_r, core == 1)
     for tap in range(27):
         a, b, cc = tap // 9, tap // 3 % 3, tap % 3
         block = wall[tap]
         rows = slice(128 * cc, 128 * cc + 128)
         wg[rows, 128 * (8 - 3 * a - b) : 128 * (9 - 3 * a - b)] = block
         wf[rows, 128 * (3 * a + b) : 128 * (3 * a + b + 1)] = block.T
-    for copy in h_copies:
-        copy.wait_recv()
+    drain(xb.at[:, :, 640:768], xh_r.at[0], has_hi)
+    drain(xb.at[:, :, 0:128], xh_r.at[1], has_lo)
 
     def patches(src, h):
         rows = [src[h + b, :, 128 * a : 128 * a + 512] for a in range(3) for b in range(3)]
@@ -232,8 +252,7 @@
         return 0
 
     lax.fori_loop(0, 4, forward, 0)
-    for copy in t_copies:
-        copy.wait_recv()
+    drain(ct.at[:, 0:112, :], t_r)
 
     up, down = row_block(lax.max(r - 1, 0)), row_block(lax.min(r + 1, 7))
     row_rims, plane_rims = [], []
@@ -258,6 +277,12 @@
         sigma = 1.0 / (1.0 + jnp.exp(-p))
         grad = ct[h].astype(F32) * sigma * (1.0 + p * (1.0 - sigma))
         gb[h + 1, :, 128:640] = grad.astype(BF16)
+        for n, at, to, dg in ((6, 128, 640, -1), (7, 512, 0, 1)):
+            has_g, from_g = (has_lo, has_hi) if dg < 0 else (has_hi, has_lo)
+            plane_rims.append(Copy(
+                gb.at[h + 1, :, at : at + 128], gb.at[h + 1, :, to : to + 128],
+                gh_s.at[n], gh_r.at[n], {"space": g + dg}, has_g, from_g,
+            ).start())
         if h == 0:
             send_rims(1, 5, has_up, has_down, up)
         if h == 3:
@@ -265,25 +290,18 @@
         gs[h, 0:128, :] = shift_lanes(grad, -1).astype(BF16)
         gs[h, 128:256, :] = grad.astype(BF16)
         gs[h, 256:384, :] = shift_lanes(grad, 1).astype(BF16)
-    plane_rims = [
-        Copy(gb.at[1:5, :, 128:256], gb.at[1:5, :, 640:768], gh_s.at[6], gh_r.at[6],
-             {"space": g - 1}, has_lo, has_hi).start(),
-        Copy(gb.at[1:5, :, 512:640], gb.at[1:5, :, 0:128], gh_s.at[7], gh_r.at[7],
-             {"space": g + 1}, has_hi, has_lo).start(),
-    ]
 
     grads = jnp.concatenate([gs[h] for h in range(4)], axis=1)
 
-    def product(ab):
-        lanes = pl.ds(pl.multiple_of(128 * lax.div(ab, 3), 128), 512)
-        rows = jnp.concatenate([xb[h + lax.rem(ab, 3), :, lanes] for h in range(4)], axis=1)
-        return lax.dot_general(rows, grads, (((1,), (1,)), ((), ())), preferred_element_type=F32)
-
-    ninth = product(jnp.int32(8))
-    for n in range(8):
-        last = ninth[:, 128 * n : 128 * n + 128] if n < 3 else jnp.zeros((128, 128), F32)
-        gw[n, 3] = last
-        gwb[n, 3] = last.astype(BF16)
+    def product(*offsets):
+        sides = []
+        for ab in offsets:
+            lanes = pl.ds(pl.multiple_of(128 * lax.div(ab, 3), 128), 512)
+            rows = [xb[h + lax.rem(ab, 3), :, lanes] for h in range(4)]
+            sides.append(jnp.concatenate(rows, axis=1))
+        side = sides[0] if len(sides) == 1 else jnp.concatenate(sides, axis=0)
+        return lax.dot_general(grads, side, (((1,), (1,)), ((), ())), preferred_element_type=F32)
+
     a_copies, b_copies = [], []
 
     def pair_sum(j):
@@ -294,23 +312,30 @@
             return total
         sb[j] = total.astype(BF16)
         b_copies.append(Copy(
-            sb.at[j], xbuf.at[j], b_s.at[j], b_r.at[j], {"space": x_peer(STEPS[j])}
+            sb.at[j], xbuf.at[j], b_s, b_r, {"space": x_peer(STEPS[j])}
         ).start())
 
     for j in range(4):
         q = lax.rem(px + STEPS[j], 4)
-        other, own = 4 * (1 - core) + q, 4 * core + q
-        prod = product(other)
+        prod = product(q, q + 4)
         for cc in range(3):
-            gwb[other, cc] = prod[:, 128 * cc : 128 * cc + 128].astype(BF16)
+            for n in range(2):
+                block = prod[128 * cc : 128 * cc + 128, 128 * n : 128 * n + 128]
+                gw[4 * n + q, cc] = block
+                gwb[4 * n + q, cc] = block.astype(BF16)
         a_copies.append(Copy(
-            gwb.at[other], abuf.at[j], a_s.at[j], a_r.at[j], {"space": sibling}
+            gwb.at[4 * (1 - core) + q], abuf.at[j], a_s, a_r.at[j], {"space": sibling}
         ).start())
-        prod = product(own)
-        for cc in range(3):
-            gw[own, cc] = prod[:, 128 * cc : 128 * cc + 128]
         if j:
             pair_sum(j - 1)
+    ninth = product(jnp.int32(8))
+    for n in range(3):
+        gw9[n] = ninth[128 * n : 128 * n + 128]
+        gwb9[n] = ninth[128 * n : 128 * n + 128].astype(BF16)
+    first = core == 0
+    a9_copy = Copy(
+        gwb9, abuf9, a9_s, a9_r, {"space": sibling}, core == 1, first
+    ).start()
 
     gi_copies = []
 
@@ -319,58 +344,80 @@
         total = shift_lanes(acc[0:128], -1) + acc[128:256] + shift_lanes(acc[256:384], 1)
         gout[h] = total.astype(BF16)
 
-    def send_rows(first, count, n):
+    def send_rows(first, count):
         for k in range(1, 8):
             to = pl.ds(pl.multiple_of(16 * chan_peer(k), 16), 16)
             gi_copies.append(Copy(
                 gout.at[pl.ds(first, count), to, :], back.at[pl.ds(4 * r + first, count)],
-                gi_s.at[7 * n + k - 1], gi_r.at[7 * n + k - 1], {"chan": chan_peer(k)},
+                gi_s, gi_r, {"chan": chan_peer(k)},
             ).start())
         back[pl.ds(4 * r + first, count)] = gout[first : first + count, mine, :]
 
-    for copy in plane_rims:
-        copy.wait_recv()
+    drain(gb.at[1:5, :, 640:768], gh_r.at[6], has_hi)
+    drain(gb.at[1:5, :, 0:128], gh_r.at[7], has_lo)
     backward(1)
     backward(2)
-    send_rows(1, 2, 0)
-
+    send_rows(1, 2)
+    a9_copy.wait_recv()
+
+    @pl.when(first)
+    def _():
+        gw9[...] = gw9[...] + abuf9[...].astype(F32)
+        sb9[...] = gw9[...].astype(BF16)
+
+    b9_copies = []
+    for k in range(1, 4):
+        q = lax.rem(px + k, 4)
+        b9_copies.append(Copy(
+            sb9.at[lax.min(q, 2)], xbuf9.at[k - 1], b9_s.at[k - 1], b9_r.at[k - 1],
+            {"space": x_peer(k)}, jnp.logical_and(first, q < 3), jnp.logical_and(first, px < 3),
+        ).start())
     for sent in row_rims:
         for copy in sent:
             copy.wait_recv()
     backward(0)
-    send_rows(0, 1, 1)
     backward(3)
-    send_rows(3, 1, 2)
 
     total = pair_sum(3)
+    drain(xbuf, b_r)
     for j in range(3):
-        b_copies[j].wait_recv()
         total = total + xbuf[j].astype(F32)
-    yb[...] = total.astype(BF16)
+    for slot in range(3):
+        yb[slot] = total[slot].T.astype(BF16)
+    yb[3] = jnp.zeros((128, 128), BF16)
+    for copy in b9_copies:
+        copy.wait_recv()
+
+    @pl.when(jnp.logical_and(first, px < 3))
+    def _():
+        total9 = gw9[lax.min(px, 2)]
+        for j in range(3):
+            total9 = total9 + xbuf9[j].astype(F32)
+        yb[3] = total9.T.astype(BF16)
+
     y_copies = []
     for dz in range(2):
         for k in range(8):
             if dz or k:
                 z, to = lax.rem(pz + dz, 2), chan_peer(k)
-                n = 8 * dz + k - 1
                 y_copies.append(Copy(
                     yb.at[:, pl.ds(pl.multiple_of(16 * to, 16), 16), :], ybuf.at[8 * pz + c],
-                    y_s.at[n], y_r.at[n], {"space": 8 * z + 2 * px + core, "chan": to},
+                    y_s, y_r, {"space": 8 * z + 2 * px + core, "chan": to},
                 ).start())
     ybuf[8 * pz + c] = yb[:, mine, :]
-    for copy in y_copies:
-        copy.wait_recv()
+    send_rows(0, 1)
+    send_rows(3, 1)
+    drain(ybuf.at[0:15], y_r)
     total = ybuf[0].astype(F32)
     for n in range(1, 16):
         total = total + ybuf[n].astype(F32)
     piece = gwf.at[4 * core + px]
     piece[...] = total.astype(BF16)
     d_copies = [
-        Copy(piece, piece, d_s.at[k - 1], d_r.at[k - 1], {"space": half_peer(k)}).start()
+        Copy(piece, piece, d_s, d_r, {"space": half_peer(k)}).start()
         for k in range(1, 8)
     ]
-    for copy in gi_copies:
-        copy.wait_recv()
+    drain(back.at[0:28], gi_r)
     for d in range(4):
         for h in range(32):
             wide[24 * h : 24 * h + 16, :] = back[h, :, 128 * d : 128 * d + 128].astype(F32)
@@ -382,18 +429,30 @@
         lax.fori_loop(0, 16, step, 0)
     out = pltpu.make_async_copy(gi_ref, gi_hbm, io_sem.at[0])
     out.start()
-    for copy in d_copies:
-        copy.wait_recv()
+    drain(fp.at[0:28], wy_s, some)
+    drain(xb.at[:, 0:112, 128:640], x_s)
+    drain(ct.at[:, 0:112, :], t_s)
+    drain(wall.at[0:12], wx_s, some)
+    drain(wall.at[0:16], wd_s, core == 0)
+    drain(wall.at[0:12], wd_s, core == 1)
+    drain(xb.at[:, :, 128:256], xh_s.at[0], has_lo)
+    drain(xb.at[:, :, 512:640], xh_s.at[1], has_hi)
+    drain(gb.at[1:5, :, 128:256], gh_s.at[6], has_lo)
+    drain(gb.at[1:5, :, 512:640], gh_s.at[7], has_hi)
+    drain(back.at[0:28], gi_s)
+    drain(gwb.at[0:4], a_s)
+    drain(sb, b_s)
+    drain(ybuf.at[0:15], y_s)
+    for copy in row_rims[0] + row_rims[1] + [a9_copy] + b9_copies:
+        copy.wait_send()
+    drain(gwf.at[0:7], d_r)
     for tap in range(27):
         n, slot = (tap // 3, tap % 3) if tap < 24 else (tap - 24, 3)
         gw_ref[tap] = gwf[n, slot].astype(F32) * scale
     out_w = pltpu.make_async_copy(gw_ref, gw_hbm, io_sem.at[1])
     out_w.start()
 
-    copies = wy_copies + x_copies + t_copies + wx_copies + wd_copies + h_copies + row_rims[0]
-    copies += row_rims[1] + plane_rims + a_copies + gi_copies + b_copies + y_copies + d_copies
-    for copy in copies:
-        copy.wait_send()
+    drain(gwf.at[0:7], d_s)
     out.wait()
     out_w.wait()
 
@@ -401,7 +460,7 @@
 def body(inputs, filters, cotangent):
     cells = inputs.shape[1] * lax.axis_size("space") * inputs.shape[2] * inputs.shape[3]
     scale = 1.0 / math.sqrt(cells)
-    pairs = [7, 7, 7, 3, 4, 2, 8, 21, 4, 3, 15, 7]
+    sems = [0, 7, 0, 0, 0, 0, 0, 3, 0, 0, 2, 2, 8, 8, 0, 0, 0, 4, 0, 0, 0, 0, 3, 3, 0, 0, 0, 0, 3]
     scratch = [
         (inputs.shape, BF16),
         (filters.shape, BF16),
@@ -420,11 +479,16 @@
         ((4, 128, 512), F32),
         ((6, 128, 768), BF16),
         ((4, 384, 512), BF16),
-        ((8, 4, 128, 128), F32),
-        ((8, 4, 128, 128), BF16),
-        ((4, 4, 128, 128), BF16),
-        ((3, 4, 128, 128), BF16),
-        ((3, 4, 128, 128), BF16),
+        ((8, 3, 128, 128), F32),
+        ((8, 3, 128, 128), BF16),
+        ((4, 3, 128, 128), BF16),
+        ((3, 3, 128, 128), BF16),
+        ((3, 3, 128, 128), BF16),
+        ((3, 128, 128), F32),
+        ((3, 128, 128), BF16),
+        ((3, 128, 128), BF16),
+        ((3, 128, 128), BF16),
+        ((3, 128, 128), BF16),
         ((4, 128, 128), BF16),
         ((16, 4, 16, 128), BF16),
         ((8, 4, 16, 128), BF16),
@@ -441,8 +505,7 @@
         in_specs=[hbm] * 3,
         out_specs=(hbm, hbm),
         scratch_shapes=[pltpu.VMEM(s, t) for s, t in scratch]
-        + [pltpu.SemaphoreType.DMA((n,)) for n in pairs for _ in range(2)]
-        + [pltpu.SemaphoreType.DMA((3,))],
+        + [pltpu.SemaphoreType.DMA((n,) if n else ()) for n in sems],
         compiler_params=pltpu.CompilerParams(
             collective_id=0, has_side_effects=True, vmem_limit_bytes=60 * 2**20
         ),

time: 60.1 us -> 59.7 us (level)
  no operation moved by 1% of the time
where the time goes in v4:
time: 59.7 us; the launch traced here: 59.5 us
  Pallas kernels  56.3 us (94%)
  local copies, waits for them, and re-layouts  2.61 us (4%)
  between operations  0.65 us (1%)
    pallas_call x1, Pallas kernels, body(): pl.pallas_call(lambda *refs: kernel(scale, *refs), out_shape=(jax.ShapeDt...  56.3 us
    unnamed x4, local copies, waits for them, and re-layouts  2.61 us

profile of v4, /device:TPU:1, one launch (start us, length us, event | category | flops | bytes accessed | tf_op | source)
XLA Modules:
  0.0 59.5 jit_solution(7610322675120518179)
XLA Ops:
  0.6 56.3 %conv_backward.1 = (bf16[16,4,32,128]{3,2,1,0:T(8,128)(2,1)}, f32[27,16,128]{2,1,0:T(8,128)}) custom-call(bf16[16,4,32,128]{3,2,1,0:T(8,128)(2,1)} %refs_0_.1, bf16[27,16,128]{2,1,0:T(8,128)(2,1)} %refs_1_.1, bf16[16,4,32,128]{3,2,1,0:T(8,128)(2,1)} %refs_2_.1), custom_call_target="tpu_custom_call" | custom-call | tf_op jit(solution)/shard_map/conv_backward/pallas_call | solution.py:499
  56.9 0.0 copy-start
  56.9 1.9 %copy.7 = bf16[16,4,32,128]{3,2,1,0:T(8,128)(2,1)} copy(bf16[16,4,32,128]{3,2,1,0:T(8,128)(2,1)} %get-tuple-element.4) | data formatting | bytes 1048576
  58.8 0.0 copy-done
  58.8 0.7 %copy.8 = f32[27,16,128]{2,1,0:T(8,128)} copy(f32[27,16,128]{2,1,0:T(8,128)S(1)} %copy-done) | data formatting | bytes 442368
Async XLA Ops:
  56.9 1.9 %copy-start = (f32[27,16,128]{2,1,0:T(8,128)S(1)}, f32[27,16,128]{2,1,0:T(8,128)}, u32[]{:S(2)}) copy-start(f32[27,16,128]{2,1,0:T(8,128)} %get-tuple-element.5) | copy-start | bytes 663556

commit v5 on v4

--- a/solution.py
+++ b/solution.py
@@ -57,7 +57,7 @@
 
 def kernel(
     scale, x_hbm, f_hbm, t_hbm, gi_hbm, gw_hbm,
-    x_ref, f_ref, t_ref, gi_ref, gw_ref, wide, xt, tt, fp, xb, ct, wall, wg, wf, pre, gb, gs, gw, gwb, abuf, sb, xbuf,
+    x_ref, f_ref, t_ref, gi_ref, gw_ref, wide, xt, tt, fp, xb, ct, wall, wg, wf, pre, xtt, gb, gs, gw, gwb, abuf, sb, xbuf,
     gw9, gwb9, abuf9, sb9, xbuf9, yb, ybuf, gwf,
     gout, back,
     x_s, x_r, t_s, t_r, wy_s, wy_r, wx_s, wx_r, wd_s, wd_r, xh_s, xh_r, gh_s, gh_r, gi_s, gi_r,
@@ -249,6 +249,10 @@
     def forward(h, _):
         acc = jnp.dot(wf[...], patches(xb, h), preferred_element_type=F32)
         pre[h] = shift_lanes(acc[0:128], 1) + acc[128:256] + shift_lanes(acc[256:384], -1)
+        for n in range(9):
+            row, plane = lax.div(9 * h + n, 6), lax.rem(9 * h + n, 6)
+            at = pl.ds(pl.multiple_of(128 * plane, 128), 128)
+            xtt[row, at, :] = xb[row, :, at].T
         return 0
 
     lax.fori_loop(0, 4, forward, 0)
@@ -297,12 +301,13 @@
         sides = []
         for ab in offsets:
             lanes = pl.ds(pl.multiple_of(128 * lax.div(ab, 3), 128), 512)
-            rows = [xb[h + lax.rem(ab, 3), :, lanes] for h in range(4)]
-            sides.append(jnp.concatenate(rows, axis=1))
-        side = sides[0] if len(sides) == 1 else jnp.concatenate(sides, axis=0)
-        return lax.dot_general(grads, side, (((1,), (1,)), ((), ())), preferred_element_type=F32)
+            rows = [xtt[h + lax.rem(ab, 3), lanes, :] for h in range(4)]
+            sides.append(jnp.concatenate(rows, axis=0))
+        side = sides[0] if len(sides) == 1 else jnp.concatenate(sides, axis=1)
+        return jnp.dot(grads, side, preferred_element_type=F32)
 
     a_copies, b_copies = [], []
+    first = core == 0
 
     def pair_sum(j):
         a_copies[j].wait_recv()
@@ -326,16 +331,30 @@
         a_copies.append(Copy(
             gwb.at[4 * (1 - core) + q], abuf.at[j], a_s, a_r.at[j], {"space": sibling}
         ).start())
+        if j == 1:
+            ninth = product(jnp.int32(8))
+            for n in range(3):
+                gw9[n] = ninth[128 * n : 128 * n + 128]
+                gwb9[n] = ninth[128 * n : 128 * n + 128].astype(BF16)
+            a9_copy = Copy(
+                gwb9, abuf9, a9_s, a9_r, {"space": sibling}, core == 1, first
+            ).start()
         if j:
             pair_sum(j - 1)
-    ninth = product(jnp.int32(8))
-    for n in range(3):
-        gw9[n] = ninth[128 * n : 128 * n + 128]
-        gwb9[n] = ninth[128 * n : 128 * n + 128].astype(BF16)
-    first = core == 0
-    a9_copy = Copy(
-        gwb9, abuf9, a9_s, a9_r, {"space": sibling}, core == 1, first
-    ).start()
+    a9_copy.wait_recv()
+
+    @pl.when(first)
+    def _():
+        gw9[...] = gw9[...] + abuf9[...].astype(F32)
+        sb9[...] = gw9[...].astype(BF16)
+
+    b9_copies = []
+    for k in range(1, 4):
+        q = lax.rem(px + k, 4)
+        b9_copies.append(Copy(
+            sb9.at[lax.min(q, 2)], xbuf9.at[k - 1], b9_s.at[k - 1], b9_r.at[k - 1],
+            {"space": x_peer(k)}, jnp.logical_and(first, q < 3), jnp.logical_and(first, px < 3),
+        ).start())
 
     gi_copies = []
 
@@ -358,20 +377,6 @@
     backward(1)
     backward(2)
     send_rows(1, 2)
-    a9_copy.wait_recv()
-
-    @pl.when(first)
-    def _():
-        gw9[...] = gw9[...] + abuf9[...].astype(F32)
-        sb9[...] = gw9[...].astype(BF16)
-
-    b9_copies = []
-    for k in range(1, 4):
-        q = lax.rem(px + k, 4)
-        b9_copies.append(Copy(
-            sb9.at[lax.min(q, 2)], xbuf9.at[k - 1], b9_s.at[k - 1], b9_r.at[k - 1],
-            {"space": x_peer(k)}, jnp.logical_and(first, q < 3), jnp.logical_and(first, px < 3),
-        ).start())
     for sent in row_rims:
         for copy in sent:
             copy.wait_recv()
@@ -477,6 +482,7 @@
         ((384, 1152), BF16),
         ((384, 1152), BF16),
         ((4, 128, 512), F32),
+        ((6, 768, 128), BF16),
         ((6, 128, 768), BF16),
         ((4, 384, 512), BF16),
         ((8, 3, 128, 128), F32),

time: 59.7 us -> 56.9 us (0.953)
  Pallas kernels: 56.3 us -> 53.4 us
    pallas_call x1, Pallas kernels: 56.3 us -> 53.4 us  [body(): pl.pallas_call(lambda *refs: kernel(scale, *refs), out_shape=(jax.ShapeDt...]
where the time goes in v5:
time: 56.9 us; the launch traced here: 56.7 us
  Pallas kernels  53.4 us (94%)
  local copies, waits for them, and re-layouts  2.61 us (5%)
  between operations  0.65 us (1%)
    pallas_call x1, Pallas kernels, body(): pl.pallas_call(lambda *refs: kernel(scale, *refs), out_shape=(jax.ShapeDt...  53.4 us
    unnamed x4, local copies, waits for them, and re-layouts  2.61 us

profile of v5, /device:TPU:1, one launch (start us, length us, event | category | flops | bytes accessed | tf_op | source)
XLA Modules:
  0.0 56.7 jit_solution(1540419710831310242)
XLA Ops:
  0.6 53.4 %conv_backward.1 = (bf16[16,4,32,128]{3,2,1,0:T(8,128)(2,1)}, f32[27,16,128]{2,1,0:T(8,128)}) custom-call(bf16[16,4,32,128]{3,2,1,0:T(8,128)(2,1)} %refs_0_.1, bf16[27,16,128]{2,1,0:T(8,128)(2,1)} %refs_1_.1, bf16[16,4,32,128]{3,2,1,0:T(8,128)(2,1)} %refs_2_.1), custom_call_target="tpu_custom_call" | custom-call | tf_op jit(solution)/shard_map/conv_backward/pallas_call | solution.py:505
  54.1 0.0 copy-start
  54.1 1.9 %copy.7 = bf16[16,4,32,128]{3,2,1,0:T(8,128)(2,1)} copy(bf16[16,4,32,128]{3,2,1,0:T(8,128)(2,1)} %get-tuple-element.4) | data formatting | bytes 1048576
  56.0 0.0 copy-done
  56.0 0.7 %copy.8 = f32[27,16,128]{2,1,0:T(8,128)} copy(f32[27,16,128]{2,1,0:T(8,128)S(1)} %copy-done) | data formatting | bytes 442368
Async XLA Ops:
  54.1 1.9 %copy-start = (f32[27,16,128]{2,1,0:T(8,128)S(1)}, f32[27,16,128]{2,1,0:T(8,128)}, u32[]{:S(2)}) copy-start(f32[27,16,128]{2,1,0:T(8,128)} %get-tuple-element.5) | copy-start | bytes 663556

commit v6 on v5

--- a/solution.py
+++ b/solution.py
@@ -460,6 +460,20 @@
     drain(gwf.at[0:7], d_s)
     out.wait()
     out_w.wait()
+
+
+def hand_over(gi_in, gw_in, gi_out, gw_out, gi, gw, sems):
+    pieces = [(gi_in.at[pl.ds(4 * n, 4)], gi.at[pl.ds(4 * n, 4)], gi_out.at[pl.ds(4 * n, 4)]) for n in range(4)]
+    pieces.append((gw_in, gw, gw_out))
+    loads = [pltpu.make_async_copy(src, mid, sems.at[0, n]) for n, (src, mid, _) in enumerate(pieces)]
+    stores = [pltpu.make_async_copy(mid, dst, sems.at[1, n]) for n, (_, mid, dst) in enumerate(pieces)]
+    for load in loads:
+        load.start()
+    for load, store in zip(loads, stores):
+        load.wait()
+        store.start()
+    for store in stores:
+        store.wait()
 
 
 def body(inputs, filters, cotangent):
@@ -502,7 +516,7 @@
         ((32, 16, 512), BF16),
     ]
     hbm = pl.BlockSpec(memory_space=pl.ANY)
-    return pl.pallas_call(
+    grads = pl.pallas_call(
         lambda *refs: kernel(scale, *refs),
         out_shape=(
             jax.ShapeDtypeStruct(inputs.shape, BF16),
@@ -517,6 +531,15 @@
         ),
         name="conv_backward",
     )(inputs, filters, cotangent)
+    return pl.pallas_call(
+        hand_over,
+        out_shape=tuple(jax.ShapeDtypeStruct(a.shape, a.dtype) for a in grads),
+        in_specs=[hbm] * 2,
+        out_specs=(hbm, hbm),
+        scratch_shapes=[pltpu.VMEM(a.shape, a.dtype) for a in grads]
+        + [pltpu.SemaphoreType.DMA((2, 5))],
+        name="hand_over",
+    )(*grads)
 
 
 def solution(mesh):

time: 56.9 us -> 56.2 us (0.988)
  local copies, waits for them, and re-layouts: 2.61 us -> 0 us
  Pallas kernels: 53.4 us -> 55.4 us
    unnamed x4 -> x0, local copies, waits for them, and re-layouts: 2.61 us -> none
    pallas_call x0 -> x1, Pallas kernels: none -> 1.97 us  [body(): pl.pallas_call(hand_over, out_shape=tuple((jax.ShapeDtypeStruct(a.shape,...]
where the time goes in v6:
time: 56.2 us; the launch traced here: 56 us
  Pallas kernels  55.4 us (99%)
  between operations  0.64 us (1%)
    pallas_call x1, Pallas kernels, body(): pl.pallas_call(lambda *refs: kernel(scale, *refs), out_shape=(jax.ShapeDt...  53.4 us
    pallas_call x1, Pallas kernels, body(): pl.pallas_call(hand_over, out_shape=tuple((jax.ShapeDtypeStruct(a.shape,...  1.97 us

profile of v6, /device:TPU:1, one launch (start us, length us, event | category | flops | bytes accessed | tf_op | source)
XLA Modules:
  0.0 56.0 jit_solution(13430010659260236707)
XLA Ops:
  0.6 53.4 %conv_backward.1 = (bf16[16,4,32,128]{3,2,1,0:T(8,128)(2,1)}, f32[27,16,128]{2,1,0:T(8,128)}) custom-call(bf16[16,4,32,128]{3,2,1,0:T(8,128)(2,1)} %refs_0_.1, bf16[27,16,128]{2,1,0:T(8,128)(2,1)} %refs_1_.1, bf16[16,4,32,128]{3,2,1,0:T(8,128)(2,1)} %refs_2_.1), custom_call_target="tpu_custom_call" | custom-call | tf_op jit(solution)/shard_map/conv_backward/pallas_call | solution.py:519
  54.1 2.0 %hand_over.1 = (bf16[16,4,32,128]{3,2,1,0:T(8,128)(2,1)}, f32[27,16,128]{2,1,0:T(8,128)}) custom-call(bf16[16,4,32,128]{3,2,1,0:T(8,128)(2,1)} %get-tuple-element.4.gi_in, f32[27,16,128]{2,1,0:T(8,128)} %get-tuple-element.5.gw_in), custom_call_target="tpu_custom_call" | custom-call | tf_op jit(solution)/shard_map/hand_over/pallas_call | solution.py:534

commit v7 on v6

--- a/solution.py
+++ b/solution.py
@@ -372,16 +372,20 @@
             ).start())
         back[pl.ds(4 * r + first, count)] = gout[first : first + count, mine, :]
 
-    drain(gb.at[1:5, :, 640:768], gh_r.at[6], has_hi)
-    drain(gb.at[1:5, :, 0:128], gh_r.at[7], has_lo)
-    backward(1)
-    backward(2)
-    send_rows(1, 2)
-    for sent in row_rims:
-        for copy in sent:
-            copy.wait_recv()
-    backward(0)
-    backward(3)
+    def finish_rows():
+        drain(gb.at[1:5, :, 640:768], gh_r.at[6], has_hi)
+        drain(gb.at[1:5, :, 0:128], gh_r.at[7], has_lo)
+        backward(1)
+        backward(2)
+        send_rows(1, 2)
+        for sent in row_rims:
+            for copy in sent:
+                copy.wait_recv()
+        backward(0)
+        backward(3)
+
+    late = g == 8
+    pl.when(jnp.logical_not(late))(finish_rows)
 
     total = pair_sum(3)
     drain(xbuf, b_r)
@@ -410,6 +414,7 @@
                     y_s, y_r, {"space": 8 * z + 2 * px + core, "chan": to},
                 ).start())
     ybuf[8 * pz + c] = yb[:, mine, :]
+    pl.when(late)(finish_rows)
     send_rows(0, 1)
     send_rows(3, 1)
     drain(ybuf.at[0:15], y_r)

time: 56.2 us -> 55.8 us (level)
  no operation moved by 1% of the time
where the time goes in v7:
time: 55.8 us; the launch traced here: 55.7 us
  Pallas kernels  55.1 us (99%)
  between operations  0.64 us (1%)
    pallas_call x1, Pallas kernels, body(): pl.pallas_call(lambda *refs: kernel(scale, *refs), out_shape=(jax.ShapeDt...  53.1 us
    pallas_call x1, Pallas kernels, body(): pl.pallas_call(hand_over, out_shape=tuple((jax.ShapeDtypeStruct(a.shape,...  1.97 us

profile of v7, /device:TPU:1, one launch (start us, length us, event | category | flops | bytes accessed | tf_op | source)
XLA Modules:
  0.0 55.7 jit_solution(12140793971484470182)
XLA Ops:
  0.6 53.1 %conv_backward.1 = (bf16[16,4,32,128]{3,2,1,0:T(8,128)(2,1)}, f32[27,16,128]{2,1,0:T(8,128)}) custom-call(bf16[16,4,32,128]{3,2,1,0:T(8,128)(2,1)} %refs_0_.1, bf16[27,16,128]{2,1,0:T(8,128)(2,1)} %refs_1_.1, bf16[16,4,32,128]{3,2,1,0:T(8,128)(2,1)} %refs_2_.1), custom_call_target="tpu_custom_call" | custom-call | tf_op jit(solution)/shard_map/conv_backward/pallas_call | solution.py:524
  53.7 2.0 %hand_over.1 = (bf16[16,4,32,128]{3,2,1,0:T(8,128)(2,1)}, f32[27,16,128]{2,1,0:T(8,128)}) custom-call(bf16[16,4,32,128]{3,2,1,0:T(8,128)(2,1)} %get-tuple-element.4.gi_in, f32[27,16,128]{2,1,0:T(8,128)} %get-tuple-element.5.gw_in), custom_call_target="tpu_custom_call" | custom-call | tf_op jit(solution)/shard_map/hand_over/pallas_call | solution.py:539

commit v8 on v7

--- a/solution.py
+++ b/solution.py
@@ -239,16 +239,24 @@
         rows = slice(128 * cc, 128 * cc + 128)
         wg[rows, 128 * (8 - 3 * a - b) : 128 * (9 - 3 * a - b)] = block
         wf[rows, 128 * (3 * a + b) : 128 * (3 * a + b + 1)] = block.T
+
+    def patches(src, h, offsets=(0, 1, 2)):
+        rows = [src[h + b, :, 128 * a : 128 * a + 512] for a in offsets for b in range(3)]
+        return jnp.concatenate(rows, axis=0)
+
+    def centre(h, _):
+        acc = jnp.dot(wf[:, 384:768], patches(xb, h, (1,)), preferred_element_type=F32)
+        pre[h] = shift_lanes(acc[0:128], 1) + acc[128:256] + shift_lanes(acc[256:384], -1)
+        return 0
+
+    lax.fori_loop(0, 4, centre, 0)
     drain(xb.at[:, :, 640:768], xh_r.at[0], has_hi)
     drain(xb.at[:, :, 0:128], xh_r.at[1], has_lo)
 
-    def patches(src, h):
-        rows = [src[h + b, :, 128 * a : 128 * a + 512] for a in range(3) for b in range(3)]
-        return jnp.concatenate(rows, axis=0)
-
     def forward(h, _):
-        acc = jnp.dot(wf[...], patches(xb, h), preferred_element_type=F32)
-        pre[h] = shift_lanes(acc[0:128], 1) + acc[128:256] + shift_lanes(acc[256:384], -1)
+        sides = jnp.concatenate([wf[:, 0:384], wf[:, 768:1152]], axis=1)
+        acc = jnp.dot(sides, patches(xb, h, (0, 2)), preferred_element_type=F32)
+        pre[h] = pre[h] + shift_lanes(acc[0:128], 1) + acc[128:256] + shift_lanes(acc[256:384], -1)
         for n in range(9):
             row, plane = lax.div(9 * h + n, 6), lax.rem(9 * h + n, 6)
             at = pl.ds(pl.multiple_of(128 * plane, 128), 128)
@@ -384,7 +392,7 @@
         backward(0)
         backward(3)
 
-    late = g == 8
+    late = jnp.logical_or(g == 7, g == 8)
     pl.when(jnp.logical_not(late))(finish_rows)
 
     total = pair_sum(3)

time: 55.8 us -> 55.8 us (level)
  no operation moved by 1% of the time
where the time goes in v8:
time: 55.8 us; the launch traced here: 55.7 us
  Pallas kernels  55 us (99%)
  between operations  0.64 us (1%)
    pallas_call x1, Pallas kernels, body(): pl.pallas_call(lambda *refs: kernel(scale, *refs), out_shape=(jax.ShapeDt...  53.1 us
    pallas_call x1, Pallas kernels, body(): pl.pallas_call(hand_over, out_shape=tuple((jax.ShapeDtypeStruct(a.shape,...  1.97 us

profile of v8, /device:TPU:1, one launch (start us, length us, event | category | flops | bytes accessed | tf_op | source)
XLA Modules:
  0.0 55.7 jit_solution(1760419597082140291)
XLA Ops:
  0.6 53.1 %conv_backward.1 = (bf16[16,4,32,128]{3,2,1,0:T(8,128)(2,1)}, f32[27,16,128]{2,1,0:T(8,128)}) custom-call(bf16[16,4,32,128]{3,2,1,0:T(8,128)(2,1)} %refs_0_.1, bf16[27,16,128]{2,1,0:T(8,128)(2,1)} %refs_1_.1, bf16[16,4,32,128]{3,2,1,0:T(8,128)(2,1)} %refs_2_.1), custom_call_target="tpu_custom_call" | custom-call | tf_op jit(solution)/shard_map/conv_backward/pallas_call | solution.py:532
  53.7 2.0 %hand_over.1 = (bf16[16,4,32,128]{3,2,1,0:T(8,128)(2,1)}, f32[27,16,128]{2,1,0:T(8,128)}) custom-call(bf16[16,4,32,128]{3,2,1,0:T(8,128)(2,1)} %get-tuple-element.4.gi_in, f32[27,16,128]{2,1,0:T(8,128)} %get-tuple-element.5.gw_in), custom_call_target="tpu_custom_call" | custom-call | tf_op jit(solution)/shard_map/hand_over/pallas_call | solution.py:547

commit v9 on v7

--- a/solution.py
+++ b/solution.py
@@ -491,7 +491,7 @@
         (inputs.shape, BF16),
         (inputs.shape, BF16),
         (filters.shape, F32),
-        ((PITCH * 16, 128), F32),
+        ((PITCH * 17, 128), F32),
         ((34, 16, 512), BF16),
         ((32, 16, 512), BF16),
         ((32, 16, 128), BF16),

time: 55.8 us -> 55.8 us (level)
  no operation moved by 1% of the time
where the time goes in v9:
time: 55.8 us; the launch traced here: 55.7 us
  Pallas kernels  55.1 us (99%)
  between operations  0.64 us (1%)
    pallas_call x1, Pallas kernels, body(): pl.pallas_call(lambda *refs: kernel(scale, *refs), out_shape=(jax.ShapeDt...  53.1 us
    pallas_call x1, Pallas kernels, body(): pl.pallas_call(hand_over, out_shape=tuple((jax.ShapeDtypeStruct(a.shape,...  1.97 us

profile of v9, /device:TPU:1, one launch (start us, length us, event | category | flops | bytes accessed | tf_op | source)
XLA Modules:
  0.0 55.7 jit_solution(17498321778801718810)
XLA Ops:
  0.6 53.1 %conv_backward.1 = (bf16[16,4,32,128]{3,2,1,0:T(8,128)(2,1)}, f32[27,16,128]{2,1,0:T(8,128)}) custom-call(bf16[16,4,32,128]{3,2,1,0:T(8,128)(2,1)} %refs_0_.1, bf16[27,16,128]{2,1,0:T(8,128)(2,1)} %refs_1_.1, bf16[16,4,32,128]{3,2,1,0:T(8,128)(2,1)} %refs_2_.1), custom_call_target="tpu_custom_call" | custom-call | tf_op jit(solution)/shard_map/conv_backward/pallas_call | solution.py:524
  53.7 2.0 %hand_over.1 = (bf16[16,4,32,128]{3,2,1,0:T(8,128)(2,1)}, f32[27,16,128]{2,1,0:T(8,128)}) custom-call(bf16[16,4,32,128]{3,2,1,0:T(8,128)(2,1)} %get-tuple-element.4.gi_in, f32[27,16,128]{2,1,0:T(8,128)} %get-tuple-element.5.gw_in), custom_call_target="tpu_custom_call" | custom-call | tf_op jit(solution)/shard_map/hand_over/pallas_call | solution.py:539
